TPU v7x, 32 devices: a whole 2x2x4 slice. The times are simulated.
32 devices in a mesh: dp: 2 (over y), seq: 8 (over z, x), head: 2 (over core).
Axes of the slice: x: 2, y: 2, z: 4, core: 2. Of those that a mesh axis runs over, the one named last changes fastest.
Arguments:
- tokens: bfloat16 [2, 2, 1024, 2048], P(None, 'dp', 'seq'), may hold values from -6 to 6
- norm_gain: float32 [2048], replicated, may hold values from 0.5 to 1.5
- w_gate_in: bfloat16 [2048, 4096], P(('dp', 'seq'), 'head'), may hold values from -0.125 to 0.125
- w_x_in: bfloat16 [2048, 4096], P(('dp', 'seq'), 'head'), may hold values from -0.125 to 0.125
- w_bc_in: bfloat16 [2048, 256], P(('dp', 'seq')), may hold values from -0.125 to 0.125
- w_dt_in: bfloat16 [2048, 64], P(('dp', 'seq'), 'head'), may hold values from -0.0625 to 0.0625
- conv_x_w: float32 [4, 4096], P(None, 'head'), may hold values from -3 to 3
- conv_x_b: float32 [4096], P('head'), may hold values from -3 to 3
- conv_bc_w: float32 [4, 256], replicated, may hold values from -3 to 3
- conv_bc_b: float32 [256], replicated, may hold values from -3 to 3
- dt_bias: float32 [64], P('head'), may hold values from -7 to -2
- a_log: float32 [64], P('head'), may hold values from 0 to 1.5
- d_skip: float32 [64], P('head'), may hold values from 0.5 to 1.5
- gate_gain: float32 [4096], P('head'), may hold values from 0.5 to 1.5
- w_out: bfloat16 [4096, 2048], P('head', ('dp', 'seq')), may hold values from -0.09375 to 0.09375
- prefix_len: int32 [2, 2], P(None, 'dp'), may hold values from 102 to 1024, as said below
- cotangent: bfloat16 [2, 2, 1024, 2048], P(None, 'dp', 'seq'), may hold values from -6 to 6
Outputs:
- result: bfloat16 [2, 2, 1024, 2048], P(None, 'dp', 'seq')
- grad_tokens: float32 [2, 2, 1024, 2048], P(None, 'dp', 'seq')
- grad_norm_gain: float32 [2048], replicated
- grad_w_gate_in: float32 [2048, 4096], P(('dp', 'seq'), 'head')
- grad_w_x_in: float32 [2048, 4096], P(('dp', 'seq'), 'head')
- grad_w_bc_in: float32 [2048, 256], P(('dp', 'seq'))
- grad_w_dt_in: float32 [2048, 64], P(('dp', 'seq'), 'head')
- grad_conv_x_w: float32 [4, 4096], P(None, 'head')
- grad_conv_x_b: float32 [4096], P('head')
- grad_conv_bc_w: float32 [4, 256], replicated
- grad_conv_bc_b: float32 [256], replicated
- grad_dt_bias: float32 [64], P('head')
- grad_a_log: float32 [64], P('head')
- grad_d_skip: float32 [64], P('head')
- grad_gate_gain: float32 [4096], P('head')
- grad_w_out: float32 [4096, 2048], P('head', ('dp', 'seq'))
Inputs may be any that keep to these rules, and one draw needn't show every extreme that they name: Tokens before a sequence's prefix_len mix both ways; some sequence has exactly 1024 and some exactly 102.
All inputs are finite; a program needn't handle non-finite values.
Results may differ from a plain program's by a relative error of at most 0.012.
Values may be sent and summed in bfloat16 or wider, within the bound.
A program may use at most 256 MiB of HBM per device.

v0:
```python
from functools import partial

import jax
import jax.numpy as jnp
from jax import lax
from jax.sharding import PartitionSpec as P

EPSILON = 1e-05
HIGHEST = lax.Precision.HIGHEST


def from_behind(block, axis, distance):
    devices = range(lax.axis_size(axis))
    route = [(i - distance, i) for i in devices if i - distance in devices]
    return lax.ppermute(block, axis, route)


def entering(part, axis, combine, identity, reverse):
    count = lax.axis_size(axis)
    place = lax.axis_index(axis)
    ahead = count - 1 - place if reverse else place
    gathered = jax.tree.map(lambda a: lax.all_gather(a, axis), part)
    state = jax.tree.map(lambda a, e: jnp.zeros_like(a) + jnp.asarray(e, a.dtype), part, identity)

    def one(step, state):
        source = count - 1 - step if reverse else step
        return combine(
            state, jax.tree.map(lambda a: lax.dynamic_index_in_dim(a, source, 0, False), gathered)
        )

    return lax.fori_loop(0, ahead, one, state)


def narrow_product(left_side, right_side):
    return jnp.dot(left_side, right_side, preferred_element_type=jnp.float32)


def rms_scale(token_rows, gain_vector):
    return (
        token_rows
        * lax.rsqrt(jnp.mean(token_rows * token_rows, axis=-1, keepdims=True) + EPSILON)
        * gain_vector
    )


def prepare(state_size, conv_ext, dt_raw, kernel, conv_bias, dt_bias, a_log):
    margin = kernel.shape[0] - 1
    length = conv_ext.shape[1] - margin
    summed = conv_bias + jnp.zeros(conv_ext[:, margin:].shape, jnp.float32)
    for offset in range(kernel.shape[0]):
        summed = summed + kernel[offset] * conv_ext[:, offset : offset + length]
    active = jax.nn.silu(summed)
    inner_width = active.shape[-1] - 2 * state_size
    head_count = dt_raw.shape[-1]
    values = active[..., :inner_width].reshape(
        active.shape[0], length, head_count, inner_width // head_count
    )
    b_input = active[..., inner_width : inner_width + state_size]
    c_output = active[..., inner_width + state_size :]
    steps_dt = jax.nn.softplus(dt_raw + dt_bias)
    cumulated = jnp.cumsum(steps_dt * -jnp.exp(a_log), axis=1)
    return (values, b_input, c_output, steps_dt, cumulated)


def elements(positions, prefix, values, b_input, steps_dt, cumulated):
    final_cum = cumulated[:, -1, :]
    carried = jnp.exp(final_cum[:, None, :] - cumulated) * steps_dt
    ends_state = jnp.einsum("sth,sthp,stn->shpn", carried, values, b_input, precision=HIGHEST)
    inside = (positions[None, :] < prefix[:, None])[:, :, None]
    opening = jnp.where(inside, jnp.exp(cumulated) * steps_dt, 0.0)
    back_state = jnp.einsum("sth,sthp,stn->shpn", opening, values, b_input, precision=HIGHEST)
    return (jnp.exp(final_cum), ends_state, back_state)


def mixer_output(
    positions, prefix, values, b_input, c_output, steps_dt, cumulated, state_in, back_in, d_skip
):
    final_cum = cumulated[:, -1, :]
    scores = jnp.einsum("stn,sun->stu", c_output, b_input, precision=HIGHEST)
    spread = cumulated[:, :, None, :] - cumulated[:, None, :, :]
    behind_mask = (positions[:, None] >= positions[None, :])[None, :, :, None]
    ahead_mask = (
        (positions[:, None] < positions[None, :])[None, :, :]
        & (positions[None, None, :] < prefix[:, None, None])
    )[..., None]
    masked = jnp.where(behind_mask, jnp.exp(jnp.where(behind_mask, spread, 0.0)), 0.0) + jnp.where(
        ahead_mask, jnp.exp(jnp.where(ahead_mask, -spread, 0.0)), 0.0
    )
    weighted = values * steps_dt[..., None]
    mixed_out = jnp.einsum(
        "stuh,suhp->sthp", scores[..., None] * masked, weighted, precision=HIGHEST
    )
    mixed_out = mixed_out + jnp.exp(cumulated)[..., None] * jnp.einsum(
        "stn,shpn->sthp", c_output, state_in, precision=HIGHEST
    )
    mixed_out = mixed_out + jnp.exp(final_cum[:, None, :] - cumulated)[..., None] * jnp.einsum(
        "stn,shpn->sthp", c_output, back_in, precision=HIGHEST
    )
    mixed_out = mixed_out + d_skip[:, None] * values
    return mixed_out.reshape(mixed_out.shape[0], mixed_out.shape[1], -1)


def gate_product(mixed_out, gate_float):
    return mixed_out * jax.nn.silu(gate_float)


def gate_norm(full_inner, gated_out, square_total, gain_vector):
    return gated_out * lax.rsqrt(square_total[..., None] / full_inner + EPSILON) * gain_vector


def chain(first_pair, second_pair):
    first_decay, first_value = first_pair
    second_decay, second_value = second_pair
    return (first_decay * second_decay, first_value * second_decay[..., None, None] + second_value)


def body(
    tokens,
    norm_gain,
    w_gate_in,
    w_x_in,
    w_bc_in,
    w_dt_in,
    conv_x_w,
    conv_x_b,
    conv_bc_w,
    conv_bc_b,
    dt_bias,
    a_log,
    d_skip,
    gate_gain,
    w_out,
    prefix_len,
    cotangent,
):
    micro_count, seq_count, length, model_width = tokens.shape
    inner_half = w_x_in.shape[1]
    state_size = w_bc_in.shape[1] // 2
    margin = conv_x_w.shape[0] - 1
    full_inner = inner_half * lax.axis_size("head")
    token_count = seq_count * length
    kernel = jnp.concatenate([conv_x_w, conv_bc_w], axis=1)
    conv_bias = jnp.concatenate([conv_x_b, conv_bc_b], axis=0)
    positions = lax.axis_index("seq") * length + jnp.arange(length, dtype=jnp.int32)

    def fetch_weights():
        return (
            lax.all_gather(w_gate_in, ("dp", "seq"), axis=0, tiled=True),
            lax.all_gather(w_x_in, ("dp", "seq"), axis=0, tiled=True),
            lax.all_gather(w_bc_in, ("dp", "seq"), axis=0, tiled=True),
            lax.all_gather(w_dt_in, ("dp", "seq"), axis=0, tiled=True),
            lax.all_gather(w_out, ("dp", "seq"), axis=1, tiled=True),
        )

    def forward_core(batch_index, weights):
        w_gate, w_inner, w_states, w_steps, w_proj = weights
        token_rows = tokens[batch_index].reshape(token_count, model_width).astype(jnp.float32)
        prefix = prefix_len[batch_index]
        normed = rms_scale(token_rows, norm_gain).astype(jnp.bfloat16)
        gate_low = narrow_product(normed, w_gate).astype(jnp.bfloat16)
        conv_input = jnp.concatenate(
            [
                narrow_product(normed, w_inner).astype(jnp.bfloat16),
                narrow_product(normed, w_states).astype(jnp.bfloat16),
            ],
            axis=1,
        ).reshape(seq_count, length, -1)
        dt_low = narrow_product(normed, w_steps).astype(jnp.bfloat16).reshape(seq_count, length, -1)
        before = from_behind(conv_input[:, length - margin :, :], "seq", 1)
        conv_ext = jnp.concatenate([before, conv_input], axis=1).astype(jnp.float32)
        dt_float = dt_low.astype(jnp.float32)
        prepared = prepare(state_size, conv_ext, dt_float, kernel, conv_bias, dt_bias, a_log)
        values, b_input, c_output, steps_dt, cumulated = prepared
        decay_rate, ends_state, back_state = elements(
            positions, prefix, values, b_input, steps_dt, cumulated
        )
        identity = (jnp.ones_like(decay_rate), jnp.zeros_like(ends_state))
        state_in = entering((decay_rate, ends_state), "seq", chain, identity, False)[1]
        back_in = entering((decay_rate, back_state), "seq", chain, identity, True)[1]
        mixed_out = mixer_output(
            positions,
            prefix,
            values,
            b_input,
            c_output,
            steps_dt,
            cumulated,
            state_in,
            back_in,
            d_skip,
        )
        gate_float = gate_low.astype(jnp.float32).reshape(seq_count, length, -1)
        gated_out = gate_product(mixed_out, gate_float)
        square_total = lax.psum(jnp.sum(gated_out * gated_out, axis=-1), "head")
        scaled = gate_norm(full_inner, gated_out, square_total, gate_gain).astype(jnp.bfloat16)
        return (
            token_rows,
            prefix,
            normed,
            gate_float,
            conv_ext,
            dt_float,
            prepared,
            decay_rate,
            state_in,
            back_in,
            mixed_out,
            gated_out,
            square_total,
            scaled,
        )

    heads_half = w_dt_in.shape[1]
    big_zero = (
        jnp.zeros((model_width, inner_half), jnp.float32),
        jnp.zeros((model_width, inner_half), jnp.float32),
        jnp.zeros((model_width, 2 * state_size), jnp.float32),
        jnp.zeros((model_width, heads_half), jnp.float32),
        jnp.zeros((inner_half, model_width), jnp.float32),
    )
    small_zero = tuple(
        (
            jnp.zeros_like(template)
            for template in (norm_gain, kernel, conv_bias, dt_bias, a_log, d_skip, gate_gain)
        )
    )
    totals = (big_zero, small_zero)
    outputs = [None] * micro_count
    grad_blocks = [None] * micro_count
    for batch_index in range(micro_count):
        weights = fetch_weights()
        forward_kept_values = forward_core(batch_index, weights)
        forward_token_rows = forward_kept_values[0]
        forward_scaled = forward_kept_values[13]
        branch = lax.psum(
            narrow_product(forward_scaled.reshape(token_count, -1), weights[4]), "head"
        )
        outputs[batch_index] = (
            (forward_token_rows + branch)
            .astype(jnp.bfloat16)
            .reshape(seq_count, length, model_width)
        )
    for batch_index in range(micro_count):
        weights = fetch_weights()
        kept_values = forward_core(batch_index, weights)
        backward_w_gate, backward_w_inner, backward_w_states, backward_w_steps, backward_w_proj = (
            weights
        )
        (
            backward_token_rows,
            backward_prefix,
            backward_normed,
            backward_gate_float,
            backward_conv_ext,
            backward_dt_float,
            backward_prepared,
            backward_decay_rate,
            backward_state_in,
            backward_back_in,
            backward_mixed_out,
            backward_gated_out,
            backward_square_total,
            backward_scaled,
        ) = kept_values
        (
            backward_values,
            backward_b_input,
            backward_c_output,
            backward_steps_dt,
            backward_cumulated,
        ) = backward_prepared
        backward_big_sums, backward_small_sums = totals
        upstream = cotangent[batch_index].reshape(token_count, model_width)
        scaled_rows = backward_scaled.reshape(token_count, -1)
        grad_proj = jnp.einsum(
            "rk,rd->kd", scaled_rows, upstream, preferred_element_type=jnp.float32
        )
        grad_scaled = jnp.einsum(
            "rd,kd->rk", upstream, backward_w_proj, preferred_element_type=jnp.float32
        ).reshape(backward_gated_out.shape)
        _, pullback = jax.vjp(
            partial(gate_norm, full_inner), backward_gated_out, backward_square_total, gate_gain
        )
        grad_gated, grad_total, backward_grad_gain = pullback(grad_scaled)
        grad_total = lax.psum(grad_total, "head")
        grad_gated = grad_gated + 2.0 * backward_gated_out * grad_total[..., None]
        _, pullback = jax.vjp(gate_product, backward_mixed_out, backward_gate_float)
        grad_mixed, grad_gate = pullback(grad_gated)
        _, pullback = jax.vjp(
            partial(mixer_output, positions, backward_prefix),
            backward_values,
            backward_b_input,
            backward_c_output,
            backward_steps_dt,
            backward_cumulated,
            backward_state_in,
            backward_back_in,
            d_skip,
        )
        (
            grad_values,
            grad_binput,
            grad_coutput,
            grad_steps,
            grad_cumul,
            grad_state,
            grad_back,
            backward_grad_skip,
        ) = pullback(grad_mixed)
        grad_identity = (jnp.ones_like(backward_decay_rate), jnp.zeros_like(grad_state))
        grad_ends = entering((backward_decay_rate, grad_state), "seq", chain, grad_identity, True)[
            1
        ]
        grad_opening = entering(
            (backward_decay_rate, grad_back), "seq", chain, grad_identity, False
        )[1]
        grad_decay = jnp.sum(grad_ends * backward_state_in, axis=(2, 3)) + jnp.sum(
            grad_opening * backward_back_in, axis=(2, 3)
        )
        _, pullback = jax.vjp(
            partial(elements, positions, backward_prefix),
            backward_values,
            backward_b_input,
            backward_steps_dt,
            backward_cumulated,
        )
        more_values, more_binput, more_steps, more_cumul = pullback(
            (grad_decay, grad_ends, grad_opening)
        )
        grad_binput, grad_coutput = lax.psum((grad_binput + more_binput, grad_coutput), "head")
        _, pullback = jax.vjp(
            partial(prepare, state_size),
            backward_conv_ext,
            backward_dt_float,
            kernel,
            conv_bias,
            dt_bias,
            a_log,
        )
        (
            grad_ext,
            grad_dtraw,
            backward_grad_kernel,
            backward_grad_cbias,
            backward_grad_dtbias,
            backward_grad_alog,
        ) = pullback(
            (
                grad_values + more_values,
                grad_binput,
                grad_coutput,
                grad_steps + more_steps,
                grad_cumul + more_cumul,
            )
        )
        returned = from_behind(grad_ext[:, :margin, :], "seq", -1)
        own_rows = grad_ext[:, margin:, :]
        own_rows = jnp.concatenate(
            [own_rows[:, : length - margin, :], own_rows[:, length - margin :, :] + returned],
            axis=1,
        ).reshape(token_count, -1)
        grad_inner = own_rows[:, :inner_half].astype(jnp.bfloat16)
        grad_states = own_rows[:, inner_half:].astype(jnp.bfloat16)
        grad_gate_low = grad_gate.reshape(token_count, -1).astype(jnp.bfloat16)
        grad_steps_low = grad_dtraw.reshape(token_count, -1).astype(jnp.bfloat16)

        def weight_grad(grad_low):
            return jnp.einsum(
                "rk,rc->kc", backward_normed, grad_low, preferred_element_type=jnp.float32
            )

        def inward(grad_low, weight_matrix):
            return jnp.einsum(
                "rc,kc->rk", grad_low, weight_matrix, preferred_element_type=jnp.float32
            )

        grad_normed = (
            inward(grad_gate_low, backward_w_gate)
            + inward(grad_inner, backward_w_inner)
            + inward(grad_steps_low, backward_w_steps)
        )
        grad_normed = lax.psum(grad_normed, "head") + inward(grad_states, backward_w_states)
        _, pullback = jax.vjp(rms_scale, backward_token_rows, norm_gain)
        grad_rows, grad_norm_gain = pullback(grad_normed)
        grad_block = (upstream.astype(jnp.float32) + grad_rows).reshape(
            seq_count, length, model_width
        )
        big_new = (
            backward_big_sums[0] + weight_grad(grad_gate_low),
            backward_big_sums[1] + weight_grad(grad_inner),
            backward_big_sums[2] + weight_grad(grad_states),
            backward_big_sums[3] + weight_grad(grad_steps_low),
            backward_big_sums[4] + grad_proj,
        )
        small_new = jax.tree.map(
            jnp.add,
            backward_small_sums,
            (
                grad_norm_gain,
                backward_grad_kernel,
                backward_grad_cbias,
                backward_grad_dtbias,
                backward_grad_alog,
                backward_grad_skip,
                backward_grad_gain,
            ),
        )
        grad_blocks[batch_index], totals = (grad_block, (big_new, small_new))
    big_sums, small_sums = totals
    grad_gate_w, grad_inner_w, grad_states_w, grad_steps_w, grad_proj_w = (
        lax.psum_scatter(big_sums[0], ("dp", "seq"), scatter_dimension=0, tiled=True),
        lax.psum_scatter(big_sums[1], ("dp", "seq"), scatter_dimension=0, tiled=True),
        lax.psum_scatter(big_sums[2], ("dp", "seq"), scatter_dimension=0, tiled=True),
        lax.psum_scatter(big_sums[3], ("dp", "seq"), scatter_dimension=0, tiled=True),
        lax.psum_scatter(big_sums[4], ("dp", "seq"), scatter_dimension=1, tiled=True),
    )
    grad_norm, grad_kernel, grad_cbias, grad_dtbias, grad_alog, grad_skip, grad_gain = lax.psum(
        (
            small_sums[0],
            small_sums[1],
            small_sums[2],
            small_sums[3],
            small_sums[4],
            small_sums[5],
            small_sums[6],
        ),
        ("dp", "seq"),
    )
    return (
        jnp.stack(outputs),
        jnp.stack(grad_blocks),
        grad_norm,
        grad_gate_w,
        grad_inner_w,
        grad_states_w,
        grad_steps_w,
        grad_kernel[:, :inner_half],
        grad_cbias[:inner_half],
        grad_kernel[:, inner_half:],
        grad_cbias[inner_half:],
        grad_dtbias,
        grad_alog,
        grad_skip,
        grad_gain,
        grad_proj_w,
    )


def solution(mesh):
    return jax.shard_map(
        body,
        mesh=mesh,
        in_specs=(
            P(None, "dp", "seq", None),
            P(),
            P(("dp", "seq"), "head"),
            P(("dp", "seq"), "head"),
            P(("dp", "seq"), None),
            P(("dp", "seq"), "head"),
            P(None, "head"),
            P("head"),
            P(),
            P(),
            P("head"),
            P("head"),
            P("head"),
            P("head"),
            P("head", ("dp", "seq")),
            P(None, "dp"),
            P(None, "dp", "seq", None),
        ),
        out_specs=(
            P(None, "dp", "seq", None),
            P(None, "dp", "seq", None),
            P(),
            P(("dp", "seq"), "head"),
            P(("dp", "seq"), "head"),
            P(("dp", "seq"), None),
            P(("dp", "seq"), "head"),
            P(None, "head"),
            P("head"),
            P(),
            P(),
            P("head"),
            P("head"),
            P("head"),
            P("head"),
            P("head", ("dp", "seq")),
        ),
        check_vma=False,
    )
```

profile of v0, /device:TPU:19, one launch (start us, length us, event | category | flops | bytes accessed | tf_op | source)
XLA Modules:
  0.0 2828.8 jit_solution(11302044778808764884)
XLA Ops:
  9.5 26.7 all_gather.48
  42.3 22.2 all-gather.23.cloned.1.call-done
  66.5 113.8 %all-gather.21.cloned.1.call-done = bf16[2048,2048]{1,0:T(8,128)(2,1)} async-done(((bf16[128,2048]{1,0:T(8,128)(2,1)}), bf16[2048,2048]{1,0:T(8,128)(2,1)}) %all-gather.21.cloned.1.call-update) | async-done | bytes 8388624 | tf_op jit(solution)/shard_map/all_gather | solution.py:149
  180.3 4.8 convolution_convert_fusion.3
  237.6 11.4 all_gather.56
  249.0 21.3 all_gather.49
  271.7 51.2 %all-gather.27.cloned.1.call-done = bf16[2048,2048]{1,0:T(8,128)(2,1)} async-done(((bf16[2048,128]{1,0:T(8,128)(2,1)}), bf16[2048,2048]{1,0:T(8,128)(2,1)}) %all-gather.27.cloned.1.call-update) | async-done | bytes 8388624 | tf_op jit(solution)/shard_map/all_gather | solution.py:152
  323.0 7.2 fusion.217
  333.7 115.2 %all-gather.35.cloned.1.call-done = f32[256,64,128]{2,1,0:T(8,128)} async-done(((f32[32,64,128]{2,1,0:T(8,128)}), f32[256,64,128]{2,1,0:T(8,128)}) %all-gather.35.cloned.1.call-update) | async-done | bytes 8388624 | tf_op jit(solution)/shard_map/all_gather | solution.py:22
  449.1 4.2 while.127
  456.1 118.6 %all-gather.33.cloned.1.call-done = f32[256,64,128]{2,1,0:T(8,128)} async-done(((f32[32,64,128]{2,1,0:T(8,128)}), f32[256,64,128]{2,1,0:T(8,128)}) %all-gather.33.cloned.1.call-update) | async-done | bytes 8388624 | tf_op jit(solution)/shard_map/all_gather | solution.py:22
  575.8 16.6 while.126
  594.9 6.7 fusion.70
  604.2 95.6 %all-gather.31.cloned.1.call-done = f32[256,64,128]{2,1,0:T(8,128)} async-done(((f32[32,64,128]{2,1,0:T(8,128)}), f32[256,64,128]{2,1,0:T(8,128)}) %all-gather.31.cloned.1.call-update) | async-done | bytes 8388624 | tf_op jit(solution)/shard_map/all_gather | solution.py:22
  700.9 7.1 while.125
  708.0 3.3 fusion.157
  711.3 113.8 %all-gather.29.cloned.1.call-done = f32[256,64,128]{2,1,0:T(8,128)} async-done(((f32[32,64,128]{2,1,0:T(8,128)}), f32[256,64,128]{2,1,0:T(8,128)}) %all-gather.29.cloned.1.call-update) | async-done | bytes 8388624 | tf_op jit(solution)/shard_map/all_gather | solution.py:22
  826.2 16.9 while.124
  845.6 6.7 fusion.79
  854.8 84.8 %all-gather.25.cloned.1.call-done = bf16[2048,2048]{1,0:T(8,128)(2,1)} async-done(((bf16[128,2048]{1,0:T(8,128)(2,1)}), bf16[2048,2048]{1,0:T(8,128)(2,1)}) %all-gather.25.cloned.1.call-update) | async-done | bytes 8388624 | tf_op jit(solution)/shard_map/all_gather | solution.py:148
  939.6 7.2 multiply_reduce_fusion.26
  947.2 3.4 multiply_reduce_fusion.27
  950.6 3.8 all-reduce.28
  955.8 8.9 multiply_reduce_fusion.13
  965.8 3.3 all-reduce.27
  970.4 6.0 fusion.141
  980.7 3.2 fusion.286
  986.6 3.2 fusion.288
  998.6 3.5 fusion.389
  1004.7 3.2 fusion.301
  1018.9 5.2 fusion.198
  1024.2 8.2 fusion.183
  1033.8 3.4 multiply_reduce_fusion.17
  1050.2 3.5 convolution_bitcast_fusion.7
  1059.4 3.2 fusion.110
  1064.3 3.6 fusion.132
  1068.8 7.9 fusion.393
  1076.7 3.9 fusion.392
  1085.2 20.5 all-gather.43.cloned.1.call-done
  1106.9 6.6 while.131
  1115.9 115.0 %all-gather.41.cloned.1.call-done = f32[256,64,128]{2,1,0:T(8,128)} async-done(((f32[32,64,128]{2,1,0:T(8,128)}), f32[256,64,128]{2,1,0:T(8,128)}) %all-gather.41.cloned.1.call-update) | async-done | bytes 8388624 | tf_op jit(solution)/shard_map/all_gather | solution.py:22
  1232.0 16.8 while.130
  1251.0 105.2 %all-gather.39.cloned.1.call-done = f32[256,64,128]{2,1,0:T(8,128)} async-done(((f32[32,64,128]{2,1,0:T(8,128)}), f32[256,64,128]{2,1,0:T(8,128)}) %all-gather.39.cloned.1.call-update) | async-done | bytes 8388624 | tf_op jit(solution)/shard_map/all_gather | solution.py:22
  1357.4 6.8 while.129
  1366.4 3.3 convolution_bitcast_fusion.5
  1375.4 105.9 %all-gather.37.cloned.1.call-done = f32[256,64,128]{2,1,0:T(8,128)} async-done(((f32[32,64,128]{2,1,0:T(8,128)}), f32[256,64,128]{2,1,0:T(8,128)}) %all-gather.37.cloned.1.call-update) | async-done | bytes 8388624 | tf_op jit(solution)/shard_map/all_gather | solution.py:22
  1482.5 17.1 while.128
  1499.6 3.5 convolution_bitcast_fusion.10
  1504.7 3.9 multiply_reduce_fusion.9
  1515.9 4.2 multiply_reduce_fusion.11
  1523.5 7.3 multiply_reduce_fusion.18
  1531.0 4.9 multiply_reduce_fusion.24
  1555.9 8.6 all-reduce.36.cloned.1.call-done
  1564.5 3.3 multiply_reduce_fusion.3
  1573.3 3.7 collective-permute-start.2
  1596.8 8.6 convolution_add_fusion.2
  1606.5 3.6 fusion.219
  1610.1 10.0 convolution_add_fusion
  1623.7 8.2 convolution_add_fusion.1
  1637.6 57.4 %all-reduce.26 = (f32[2048]{0:T(1024)}, f32[4,2304]{1,0:T(4,128)S(1)}, f32[2304]{0:T(1024)S(1)}, f32[32]{0:T(128)}, f32[32]{0:T(128)}, /*index=5*/f32[32]{0:T(128)}, f32[2048]{0:T(1024)}) all-reduce(f32[2048]{0:T(1024)S(1)} %add.736, f32[4,2304]{1,0:T(4,128)S(1)} %add_add_fusion.4, ...), channel_id=1, replica_groups=mesh['dp'=2,'seq'=8,'head'=2] {'dp','seq'}, use_global_device_ids=true, to_apply=%region_62.64 | all-reduce | flops 15712 | bytes 125696 | tf_op jit(solution)/shard_map/psum | solution.py:417
  1702.9 59.0 %reduce-scatter.10.cloned.1.call-done = f32[128,256]{1,0:T(8,128)} async-done(((f32[2048,256]{1,0:T(8,128)}), f32[128,256]{1,0:T(8,128)}) %reduce-scatter.10.cloned.1.call-update) | async-done | bytes 131088 | tf_op jit(solution)/shard_map/reduce_scatter | solution.py:413
  1761.9 361.6 %reduce-scatter.6.cloned.1.call-done = f32[128,2048]{1,0:T(8,128)} async-done(((f32[2048,2048]{1,0:T(8,128)}), f32[128,2048]{1,0:T(8,128)}) %reduce-scatter.6.cloned.1.call-update) | async-done | bytes 1048592 | tf_op jit(solution)/shard_map/reduce_scatter | solution.py:411
  2123.5 349.3 %reduce-scatter.14.cloned.1.call-done = f32[2048,128]{1,0:T(8,128)} async-done(((f32[2048,2048]{1,0:T(8,128)}), f32[2048,128]{1,0:T(8,128)}) %reduce-scatter.14.cloned.1.call-update) | async-done | bytes 1048592 | tf_op jit(solution)/shard_map/reduce_scatter | solution.py:415
  2472.7 349.4 %reduce-scatter.8.cloned.1.call-done = f32[128,2048]{1,0:T(8,128)} async-done(((f32[2048,2048]{1,0:T(8,128)}), f32[128,2048]{1,0:T(8,128)}) %reduce-scatter.8.cloned.1.call-update) | async-done | bytes 1048592 | tf_op jit(solution)/shard_map/reduce_scatter | solution.py:412
  (700 shorter events, 326.9 us)
Async XLA Ops:
  7.2 29.0 %copy-start.12 = (bf16[2,1,128,2048]{3,2,1,0:T(8,128)(2,1)S(1)}, bf16[2,1,128,2048]{3,2,1,0:T(8,128)(2,1)}, u32[]{:S(2)}) copy-start(bf16[2,1,128,2048]{3,2,1,0:T(8,128)(2,1)} %param.34) | copy-start | bytes 3145732
  7.2 29.8 %copy-start.191 = (f32[32]{0:T(128)S(1)}, f32[32]{0:T(128)}, u32[]{:S(2)}) copy-start(f32[32]{0:T(128)} %param.45) | copy-start | bytes 388
  7.2 29.8 %copy-start.59 = (f32[2048]{0:T(1024)S(1)}, f32[2048]{0:T(1024)}, u32[]{:S(2)}) copy-start(f32[2048]{0:T(1024)} %param.35) | copy-start | bytes 24580
  7.2 29.8 %copy-start.194 = (f32[32]{0:T(128)S(1)}, f32[32]{0:T(128)}, u32[]{:S(2)}) copy-start(f32[32]{0:T(128)} %param.44) | copy-start | bytes 388
  7.2 57.2 %all-gather.23.cloned.1.call-start = ((), (), s32[]{:S(2)}) async-start(), calls=%async_computation.6 | async-start | bytes 1114112 | tf_op jit(solution)/shard_map/all_gather | solution.py:150
  8.0 172.3 %all-gather.21.cloned.1.call-start = ((), (), s32[]{:S(2)}) async-start(), calls=%async_computation.5 | async-start | bytes 8912896 | tf_op jit(solution)/shard_map/all_gather | solution.py:149
  8.7 314.3 %all-gather.27.cloned.1.call-start = ((), (), s32[]{:S(2)}) async-start(), calls=%async_computation.8 | async-start | bytes 8912896 | tf_op jit(solution)/shard_map/all_gather | solution.py:152
  9.4 439.5 %all-gather.35.cloned.1.call-start = ((), (), s32[]{:S(2)}) async-start(), calls=%async_computation.17 | async-start | bytes 9437184 | tf_op jit(solution)/shard_map/all_gather | solution.py:22
  37.0 143.3 %copy-start.135 = (f32[128]{0:T(128)}, f32[128]{0:T(128)S(1)}, u32[]{:S(2)}) copy-start(f32[128]{0:T(128)S(1)} %fusion.355) | copy-start | bytes 1540
  37.0 151.1 %copy-start.138 = (f32[128]{0:T(128)}, f32[128]{0:T(128)S(1)}, u32[]{:S(2)}) copy-start(f32[128]{0:T(128)S(1)} %fusion.356) | copy-start | bytes 1540
  37.9 28.2 copy-start.70
  38.8 27.3 copy-start.62
  42.2 152.4 %copy-start.108 = (f32[2304]{0:T(1024)}, f32[2304]{0:T(1024)S(1)}, u32[]{:S(2)}) copy-start(f32[2304]{0:T(1024)S(1)} %get-tuple-element.872) | copy-start | bytes 27652
  42.2 152.4 %copy-start.110 = (f32[2304]{0:T(1024)}, f32[2304]{0:T(1024)S(1)}, u32[]{:S(2)}) copy-start(f32[2304]{0:T(1024)S(1)} %get-tuple-element.873) | copy-start | bytes 27652
  42.2 152.4 %copy-start.112 = (f32[2304]{0:T(1024)}, f32[2304]{0:T(1024)S(1)}, u32[]{:S(2)}) copy-start(f32[2304]{0:T(1024)S(1)} %get-tuple-element.874) | copy-start | bytes 27652
  42.2 152.4 %copy-start.114 = (f32[2304]{0:T(1024)}, f32[2304]{0:T(1024)S(1)}, u32[]{:S(2)}) copy-start(f32[2304]{0:T(1024)S(1)} %get-tuple-element.875) | copy-start | bytes 27652
  180.3 7.8 copy-start
  185.2 7.3 collective-permute-start
  189.6 4.9 collective-permute-start.1
  203.8 370.9 %all-gather.33.cloned.1.call-start = ((), (), s32[]{:S(2)}) async-start(), calls=%async_computation.16 | async-start | bytes 9437184 | tf_op jit(solution)/shard_map/all_gather | solution.py:22
  208.2 491.6 %all-gather.31.cloned.1.call-start = ((), (), s32[]{:S(2)}) async-start(), calls=%async_computation.15 | async-start | bytes 9437184 | tf_op jit(solution)/shard_map/all_gather | solution.py:22
  220.1 604.9 %all-gather.29.cloned.1.call-start = ((), (), s32[]{:S(2)}) async-start(), calls=%async_computation.14 | async-start | bytes 9437184 | tf_op jit(solution)/shard_map/all_gather | solution.py:22
  224.8 714.8 %all-gather.25.cloned.1.call-start = ((), (), s32[]{:S(2)}) async-start(), calls=%async_computation.7 | async-start | bytes 8912896 | tf_op jit(solution)/shard_map/all_gather | solution.py:148
  225.6 880.2 %all-gather.43.cloned.1.call-start = ((), (), s32[]{:S(2)}) async-start(), calls=%async_computation.21 | async-start | bytes 9437184 | tf_op jit(solution)/shard_map/all_gather | solution.py:22
  234.9 88.1 %copy-start.31 = (bf16[2,1,128,2048]{3,2,1,0:T(8,128)(2,1)S(1)}, bf16[2,1,128,2048]{3,2,1,0:T(8,128)(2,1)}, u32[]{:S(2)}) copy-start(bf16[2,1,128,2048]{3,2,1,0:T(8,128)(2,1)} %param.50) | copy-start | bytes 3145732
  939.6 7.5 copy-start.54
  939.6 7.5 copy-start.60
  939.6 7.5 copy-start.136
  955.1 9.6 copy-start.148
  955.8 9.0 copy-start.145
  955.8 9.0 copy-start.199
  955.8 9.5 copy-start.198
  984.0 246.9 %all-gather.41.cloned.1.call-start = ((), (), s32[]{:S(2)}) async-start(), calls=%async_computation.20 | async-start | bytes 9437184 | tf_op jit(solution)/shard_map/all_gather | solution.py:22
  989.8 366.4 %all-gather.39.cloned.1.call-start = ((), (), s32[]{:S(2)}) async-start(), calls=%async_computation.19 | async-start | bytes 9437184 | tf_op jit(solution)/shard_map/all_gather | solution.py:22
  1007.9 473.4 %all-gather.37.cloned.1.call-start = ((), (), s32[]{:S(2)}) async-start(), calls=%async_computation.18 | async-start | bytes 9437184 | tf_op jit(solution)/shard_map/all_gather | solution.py:22
  1013.7 550.7 %all-reduce.36.cloned.1.call-start = ((), (), s32[]{:S(2)}) async-start(), calls=%async_computation.23 | async-start | bytes 524288 | tf_op jit(solution)/shard_map/psum | solution.py:330
  1053.8 10.5 copy-start.33
  1059.4 17.3 slice-start.4
  1064.3 12.3 slice-start.5
  1067.9 8.7 copy-start.44
  1068.8 11.8 slice-start
  1520.9 17.4 copy-start.78
  1521.7 16.5 copy-start.81
  1522.6 17.2 copy-start.79
  1523.4 16.4 copy-start.82
  1523.4 7.4 copy-start.25
  1523.4 7.4 copy-start.48
  1523.4 7.4 copy-start.56
  1523.5 7.4 copy-start.80
  1523.5 7.4 copy-start.103
  1523.5 7.4 copy-start.105
  1523.5 7.4 copy-start.124
  1538.2 95.2 %all-reduce.34.cloned.1.call-start = ((), (), s32[]{:S(2)}) async-start(), calls=%async_computation.22 | async-start | bytes 8388608 | tf_op jit(solution)/shard_map/psum | solution.py:235
  1570.5 6.7 collective-permute-start.3
  1573.3 9.4 collective-permute-start.2
  1578.5 12.9 copy-start.37
  1588.2 114.6 %reduce-scatter.12.cloned.1.call-start = ((), (), s32[]{:S(2)}) async-start(), calls=%async_computation.12 | async-start | bytes 278528 | tf_op jit(solution)/shard_map/reduce_scatter | solution.py:414
  1590.8 171.1 %reduce-scatter.10.cloned.1.call-start = ((), (), s32[]{:S(2)}) async-start(), calls=%async_computation.11 | async-start | bytes 2228224 | tf_op jit(solution)/shard_map/reduce_scatter | solution.py:413
  1593.3 530.2 %reduce-scatter.6.cloned.1.call-start = ((), (), s32[]{:S(2)}) async-start(), calls=%async_computation.9 | async-start | bytes 17825792 | tf_op jit(solution)/shard_map/reduce_scatter | solution.py:411
  1605.4 867.4 %reduce-scatter.14.cloned.1.call-start = ((), (), s32[]{:S(2)}) async-start(), calls=%async_computation.13 | async-start | bytes 17825792 | tf_op jit(solution)/shard_map/reduce_scatter | solution.py:415
  1620.2 1201.9 %reduce-scatter.8.cloned.1.call-start = ((), (), s32[]{:S(2)}) async-start(), calls=%async_computation.10 | async-start | bytes 17825792 | tf_op jit(solution)/shard_map/reduce_scatter | solution.py:412
  1635.7 61.7 %copy-start.173 = (f32[128]{0:T(128)S(1)}, f32[128]{0:T(128)}, u32[]{:S(2)}) copy-start(f32[128]{0:T(128)} %copy-done.172) | copy-start | bytes 1540
  1635.7 61.7 %copy-start.175 = (f32[128]{0:T(128)S(1)}, f32[128]{0:T(128)}, u32[]{:S(2)}) copy-start(f32[128]{0:T(128)} %copy-done.174) | copy-start | bytes 1540
  1635.7 61.7 %copy-start.32 = (bf16[2,1,128,2048]{3,2,1,0:T(8,128)(2,1)S(1)}, bf16[2,1,128,2048]{3,2,1,0:T(8,128)(2,1)}, u32[]{:S(2)}) copy-start(bf16[2,1,128,2048]{3,2,1,0:T(8,128)(2,1)} %param.50) | copy-start | bytes 3145732
  (165 other events, 586.0 us)
Sparse Core Ops, SparseCore 0:
  10.9 53.5 all-gather.22
  67.3 112.9 all-gather.20
  183.0 139.9 all-gather.26
  325.5 123.3 all-gather.34
  451.5 123.1 all-gather.32
  576.6 123.1 all-gather.30
  701.9 123.1 all-gather.28
  827.9 111.7 all-gather.24
  984.1 121.6 all-gather.42
  1107.8 123.1 all-gather.40
  1233.1 123.1 all-gather.38
  1358.2 123.1 all-gather.36
  1538.3 26.0 all-reduce.35
  1588.3 30.4 all-reduce.33
  1621.5 58.5 reduce-scatter.11
  1682.9 78.8 reduce-scatter.9
  1764.7 358.7 reduce-scatter.5
  2126.3 346.4 reduce-scatter.13
  2475.7 346.3 reduce-scatter.7
where the time goes:
time: 2840 us; the launch traced here: 2830 us
  waiting for transfers between devices  2190 us (77%)
  matrix products  223 us (8%)
  other arithmetic  141 us (5%)
  blocking collectives  124 us (4%)
  local copies, waits for them, and re-layouts  116 us (4%)
    all_gather x8, waiting for transfers between devices, entering(): gathered = jax.tree.map(lambda a: lax.all_gather(a, axis), part)  790 us
    reduce_scatter x1, waiting for transfers between devices, body(): lax.psum_scatter(big_sums[0], ('dp', 'seq'), scatter_dimension=0, tiled=T...  362 us
    reduce_scatter x1, waiting for transfers between devices, body(): lax.psum_scatter(big_sums[1], ('dp', 'seq'), scatter_dimension=0, tiled=T...  349 us
    reduce_scatter x1, waiting for transfers between devices, body(): lax.psum_scatter(big_sums[4], ('dp', 'seq'), scatter_dimension=1, tiled=T...  349 us
    all_gather x1, waiting for transfers between devices, fetch_weights(): lax.all_gather(w_x_in, ('dp', 'seq'), axis=0, tiled=True)  114 us
    all_gather x1, waiting for transfers between devices, fetch_weights(): lax.all_gather(w_gate_in, ('dp', 'seq'), axis=0, tiled=True)  84.8 us
    add x28, other arithmetic, chain(): first_value * second_decay[..., None, None] + second_value  73.5 us
    reduce_scatter x1, waiting for transfers between devices, body(): lax.psum_scatter(big_sums[2], ('dp', 'seq'), scatter_dimension=0, tiled=T...  59 us
  transfers between devices with their start and end apart: 23, of which 18 were waited for; matrix products, arithmetic and copies ran while one was open for 13% of the time, Pallas kernels for 0%

commit v1 on v0

v1 whole, which is shorter than its diff:
```python
import jax
import jax.numpy as jnp
from jax import lax
from jax.sharding import PartitionSpec as P

EPSILON = 1e-05
HIGHEST = lax.Precision.HIGHEST
BF16 = jnp.bfloat16
F32 = jnp.float32
CHUNK = 128


def dot_f32(a, b):
    return jnp.dot(a, b, preferred_element_type=F32)


def causal_conv(signal, kernel, bias):
    margin = kernel.shape[0] - 1
    length = signal.shape[1]
    padded = jnp.pad(signal, ((0, 0), (margin, 0), (0, 0)))
    summed = bias + jnp.zeros_like(signal)
    for offset in range(kernel.shape[0]):
        summed = summed + kernel[offset] * padded[:, offset : offset + length]
    return summed


def mixer(prefix, inner, bc, dt_raw, conv_x_w, conv_x_b, conv_bc_w, conv_bc_b, dt_bias, a_log, d_skip):
    seqs, length, width = inner.shape
    heads = dt_raw.shape[-1]
    state = bc.shape[-1] // 2
    chunk = CHUNK
    count = length // chunk
    values = jax.nn.silu(causal_conv(inner, conv_x_w, conv_x_b))
    active = jax.nn.silu(causal_conv(bc, conv_bc_w, conv_bc_b))
    values = values.reshape(seqs, count, chunk, heads, width // heads)
    b_in = active[..., :state].reshape(seqs, count, chunk, state)
    c_out = active[..., state:].reshape(seqs, count, chunk, state)
    dt = jax.nn.softplus(dt_raw + dt_bias).reshape(seqs, count, chunk, heads)
    cum = jnp.cumsum(dt * -jnp.exp(a_log), axis=2)
    end = cum[:, :, -1:, :]
    places = jnp.arange(length, dtype=jnp.int32).reshape(count, chunk)
    inside = (places[None] < prefix[:, None, None])[..., None]
    weighted = values * dt[..., None]
    ends_state = jnp.einsum("skth,skthp,sktn->skhpn", jnp.exp(end - cum), weighted, b_in, precision=HIGHEST)
    back_state = jnp.einsum(
        "skth,skthp,sktn->skhpn", jnp.where(inside, jnp.exp(cum), 0.0), weighted, b_in, precision=HIGHEST
    )
    decay = jnp.exp(end[:, :, 0])[..., None, None]
    zero = jnp.zeros_like(ends_state[:, 0])
    state_in, back_in = [zero], [zero]
    for k in range(count - 1):
        state_in.append(state_in[-1] * decay[:, k] + ends_state[:, k])
        back_in.append(back_in[-1] * decay[:, count - 1 - k] + back_state[:, count - 1 - k])
    state_in = jnp.stack(state_in, axis=1)
    back_in = jnp.stack(back_in[::-1], axis=1)
    scores = jnp.einsum("sktn,skun->sktu", c_out, b_in, precision=HIGHEST)
    spread = cum[:, :, :, None, :] - cum[:, :, None, :, :]
    behind = (places[:, :, None] >= places[:, None, :])[None, ..., None]
    ahead = ((places[:, :, None] < places[:, None, :])[None] & (places[None, :, None, :] < prefix[:, None, None, None]))[
        ..., None
    ]
    masked = jnp.where(behind, jnp.exp(jnp.where(behind, spread, 0.0)), 0.0) + jnp.where(
        ahead, jnp.exp(jnp.where(ahead, -spread, 0.0)), 0.0
    )
    out = jnp.einsum("sktuh,skuhp->skthp", scores[..., None] * masked, weighted, precision=HIGHEST)
    out = out + jnp.exp(cum)[..., None] * jnp.einsum("sktn,skhpn->skthp", c_out, state_in, precision=HIGHEST)
    out = out + jnp.exp(end - cum)[..., None] * jnp.einsum("sktn,skhpn->skthp", c_out, back_in, precision=HIGHEST)
    out = out + d_skip[:, None] * values
    return out.reshape(seqs, length, width)


def body(
    tokens, norm_gain, w_gate_in, w_x_in, w_bc_in, w_dt_in, conv_x_w, conv_x_b, conv_bc_w, conv_bc_b,
    dt_bias, a_log, d_skip, gate_gain, w_out, prefix_len, cotangent,
):
    dp, sq, hd = lax.axis_size("dp"), lax.axis_size("seq"), lax.axis_size("head")
    me_seq, me_head = lax.axis_index("seq"), lax.axis_index("head")
    micro, seqs, span, model = tokens.shape
    group = micro * seqs
    length = span * sq
    rows_here = group * span
    own_rows = rows_here // hd
    half = w_x_in.shape[1]
    width = half // sq
    heads = w_dt_in.shape[1] // sq
    full_inner = half * hd
    prefix = prefix_len.reshape(group)
    everyone = ("seq", "head")

    def mine(x):
        return lax.dynamic_slice_in_dim(x.reshape(rows_here, model), me_head * own_rows, own_rows, 0)

    def to_sequences(x):
        return x.reshape(sq, group, span, -1).transpose(1, 0, 2, 3).reshape(group, length, -1)

    def from_sequences(x):
        return x.reshape(group, sq, span, -1).transpose(1, 0, 2, 3).reshape(sq * rows_here, -1)

    def rms(x, gain):
        return x * lax.rsqrt(jnp.mean(x * x, axis=-1, keepdims=True) + EPSILON) * gain

    my_tokens = mine(tokens).astype(F32)
    my_cot = mine(cotangent)
    normed_own = rms(my_tokens, norm_gain).astype(BF16)
    normed = lax.all_gather(normed_own, everyone, axis=0, tiled=True)

    def columns(w):
        return lax.all_gather(
            lax.all_to_all(w, "seq", split_axis=1, concat_axis=0, tiled=True), "dp", axis=0, tiled=True
        )

    wg = columns(w_gate_in)
    wx = columns(w_x_in)
    wd = lax.dynamic_slice_in_dim(
        lax.all_gather(w_dt_in, ("dp", "seq"), axis=0, tiled=True), me_seq * heads, heads, 1
    )
    wb = lax.all_gather(w_bc_in, ("dp", "seq"), axis=0, tiled=True)
    wo = lax.all_gather(
        lax.all_to_all(w_out, "seq", split_axis=0, concat_axis=1, tiled=True), "dp", axis=1, tiled=True
    )
    cot = lax.all_gather(my_cot, everyone, axis=0, tiled=True)

    def part(x, size, axis):
        return lax.dynamic_slice_in_dim(x, me_seq * size, size, axis)

    cxw, cxb = part(conv_x_w, width, 1), part(conv_x_b, width, 0)
    dtb, alog, dsk = part(dt_bias, heads, 0), part(a_log, heads, 0), part(d_skip, heads, 0)
    gain = part(gate_gain, width, 0)

    def project(w):
        return to_sequences(dot_f32(normed, w).astype(BF16)).astype(F32)

    gate, inner, bc, dt_raw = project(wg), project(wx), project(wb), project(wd)
    mixed, pull = jax.vjp(
        lambda *a: mixer(prefix, *a), inner, bc, dt_raw, cxw, cxb, conv_bc_w, conv_bc_b, dtb, alog, dsk
    )
    sig = jax.nn.sigmoid(gate)
    act = gate * sig
    gated = mixed * act
    grad_scaled = to_sequences(
        jnp.einsum("rd,kd->rk", cot, wo, preferred_element_type=F32)
    )
    gs = grad_scaled * gain
    sums = lax.psum(
        jnp.stack([jnp.sum(gated * gated, axis=-1), jnp.sum(gs * gated, axis=-1)]), everyone
    )
    scale = lax.rsqrt(sums[0][..., None] / full_inner + EPSILON)
    unit = gated * scale
    scaled = from_sequences((unit * gain).astype(BF16))
    branch = lax.psum_scatter(
        dot_f32(scaled, wo).astype(BF16), everyone, scatter_dimension=0, tiled=True
    )
    result_own = (my_tokens + branch.astype(F32)).astype(BF16)
    grad_gain = jnp.sum(grad_scaled * unit, axis=(0, 1))
    grad_wo = jnp.einsum("rk,rd->kd", scaled, cot, preferred_element_type=F32)
    grad_gated = gs * scale - gated * (scale * scale * scale * (sums[1][..., None] / full_inner))
    grad_mixed = grad_gated * act
    grad_gate = grad_gated * mixed * (sig * (1.0 + gate * (1.0 - sig)))
    d_inner, d_bc, d_dt, d_cxw, d_cxb, d_cbw, d_cbb, d_dtb, d_alog, d_dsk = pull(grad_mixed)
    gg = from_sequences(grad_gate.astype(BF16))
    gx = from_sequences(d_inner.astype(BF16))
    gd = from_sequences(d_dt.astype(BF16))
    gb_own = lax.psum_scatter(from_sequences(d_bc), everyone, scatter_dimension=0, tiled=True).astype(BF16)

    def inward(g, w):
        return jnp.einsum("rc,kc->rk", g, w, preferred_element_type=F32)

    def weight_grad(n, g):
        return jnp.einsum("rk,rc->kc", n, g, preferred_element_type=F32)

    part_normed = inward(gg, wg) + inward(gx, wx) + inward(gd, wd)
    grad_normed = lax.psum_scatter(
        part_normed.astype(BF16), everyone, scatter_dimension=0, tiled=True
    ).astype(F32) + inward(gb_own, wb)
    _, pull_norm = jax.vjp(rms, my_tokens, norm_gain)
    grad_rows, grad_norm = pull_norm(grad_normed)
    grad_own = my_cot.astype(F32) + grad_rows

    def home(g):
        return lax.all_to_all(
            lax.psum_scatter(g.astype(BF16), "dp", scatter_dimension=0, tiled=True),
            "seq", split_axis=0, concat_axis=1, tiled=True,
        ).astype(F32)

    g_gate, g_x = home(weight_grad(normed, gg)), home(weight_grad(normed, gx))
    g_dt = lax.all_to_all(
        lax.psum_scatter(weight_grad(normed, gd), "dp", scatter_dimension=0, tiled=True),
        "seq", split_axis=0, concat_axis=1, tiled=True,
    )
    g_bc = lax.psum_scatter(
        lax.psum(weight_grad(normed_own, gb_own), "head"), ("dp", "seq"), scatter_dimension=0, tiled=True
    )
    g_out = lax.all_to_all(
        lax.psum_scatter(grad_wo.astype(BF16), "dp", scatter_dimension=1, tiled=True),
        "seq", split_axis=1, concat_axis=0, tiled=True,
    ).astype(F32)

    def whole(x):
        return lax.all_gather(x, "head", axis=0, tiled=True).reshape(micro, seqs, span, model)

    small = lax.psum((d_cxw, d_cxb, d_dtb, d_alog, d_dsk, grad_gain), "dp")
    small = [lax.all_gather(a, "seq", axis=a.ndim - 1, tiled=True) for a in small]
    grad_norm, d_cbw, d_cbb = lax.psum((grad_norm, d_cbw, d_cbb), ("dp", "seq", "head"))
    return (
        whole(result_own), whole(grad_own), grad_norm, g_gate, g_x, g_bc, g_dt,
        small[0], small[1], d_cbw, d_cbb, small[2], small[3], small[4], small[5], g_out,
    )


def solution(mesh):
    rows = P(("dp", "seq"), "head")
    tok = P(None, "dp", "seq", None)
    return jax.shard_map(
        body,
        mesh=mesh,
        in_specs=(
            tok, P(), rows, rows, P(("dp", "seq"), None), rows, P(None, "head"), P("head"), P(), P(),
            P("head"), P("head"), P("head"), P("head"), P("head", ("dp", "seq")), P(None, "dp"), tok,
        ),
        out_specs=(
            tok, tok, P(), rows, rows, P(("dp", "seq"), None), rows, P(None, "head"), P("head"), P(), P(),
            P("head"), P("head"), P("head"), P("head"), P("head", ("dp", "seq")),
        ),
        check_vma=False,
    )
```

time: 2840 us -> 1110 us (0.39)
  waiting for transfers between devices: 2190 us -> 390 us
  blocking collectives: 124 us -> 277 us
  matrix products: 223 us -> 176 us
  local copies, waits for them, and re-layouts: 116 us -> 72 us
    all_gather x12 -> x8, waiting for transfers between devices: 1060 us -> 111 us  [the longest x1 76.2 us: body(): cot = lax.all_gather(my_cot, everyone, axis=0, tiled=True)]
    reduce_scatter x5 -> x7, waiting for transfers between devices: 1120 us -> 257 us  [the longest x1 107 us: body(): lax.psum_scatter(dot_f32(scaled, wo).astype(BF16), everyone, scatter_dime...]
    another operation x9 -> x5, other arithmetic: 11.9 us -> 95.8 us  [the longest x2 94.9 us: mixer(): cum = jnp.cumsum(dt * -jnp.exp(a_log), axis=2)]
    add x40 -> x2, other arithmetic: 76.6 us -> 2.85 us  [the longest x1 2.59 us: body(): grad_own = my_cot.astype(F32) + grad_rows]
    all_to_all x0 -> x3, blocking collectives: none -> 55.7 us  [the longest x1 25.3 us: body(): lax.all_to_all(w_out, 'seq', split_axis=0, concat_axis=1, tiled=True)]
    dot_general x66 -> x32, matrix products: 223 us -> 169 us  [the longest x4 34.6 us: inward(): return jnp.einsum('rc,kc->rk', g, w, preferred_element_type=F32)]
    mul x44 -> x3, local copies, waits for them, and re-layouts: 51.5 us -> 1.68 us  [the longest x1 0.66 us: body(): gs = grad_scaled * gain]
    psum x3, blocking collectives: 64.4 us -> 111 us  [the longest x1 56.5 us: body(): lax.psum((grad_norm, d_cbw, d_cbb), ('dp', 'seq', 'head'))]
  transfers between devices with their start and end apart: 23 -> 21, of which waited for: 18 -> 10; matrix products, arithmetic and copies ran while one was open for 13% -> 16% of each run, Pallas kernels for 0% -> 0%
where the time goes in v1:
time: 1110 us; the launch traced here: 1100 us
  waiting for transfers between devices  390 us (35%)
  blocking collectives  277 us (25%)
  matrix products  176 us (16%)
  other arithmetic  145 us (13%)
  local copies, waits for them, and re-layouts  72 us (6%)
  starting transfers between devices  28.2 us (3%)
  between operations  16.4 us (1%)
    reduce_scatter x1, waiting for transfers between devices, body(): lax.psum_scatter(dot_f32(scaled, wo).astype(BF16), everyone, scatter_dime...  107 us
    reduce_scatter x1, waiting for transfers between devices, body(): lax.psum_scatter(part_normed.astype(BF16), everyone, scatter_dimension=0,...  103 us
    another operation x2, other arithmetic, mixer(): cum = jnp.cumsum(dt * -jnp.exp(a_log), axis=2)  94.9 us
    all_gather x1, waiting for transfers between devices, body(): cot = lax.all_gather(my_cot, everyone, axis=0, tiled=True)  76.2 us
    psum x1, blocking collectives, body(): lax.psum((grad_norm, d_cbw, d_cbb), ('dp', 'seq', 'head'))  56.5 us
    all_gather x3, blocking collectives, body(): lax.all_gather(a, 'seq', axis=a.ndim - 1, tiled=True)  54.6 us
    psum x1, blocking collectives, body(): lax.psum(jnp.stack([jnp.sum(gated * gated, axis=-1), jnp.sum(gs * gated,...  50.2 us
    all_gather x1, blocking collectives, body(): lax.all_gather(w_dt_in, ('dp', 'seq'), axis=0, tiled=True)  38.6 us
  transfers between devices with their start and end apart: 21, of which 10 were waited for; matrix products, arithmetic and copies ran while one was open for 16% of the time, Pallas kernels for 0%

profile of v1, /device:TPU:19, one launch (start us, length us, event | category | flops | bytes accessed | tf_op | source)
XLA Modules:
  0.0 1103.3 jit_solution(2029383470495228353)
XLA Ops:
  12.0 22.4 %all_to_all.115 = bf16[128,8,256]{0,2,1:T(8,128)(2,1)S(1)} all-to-all(bf16[128,8,256]{0,2,1:T(8,128)(2,1)S(1)} %bitcast.572), channel_id=1, replica_groups=mesh['dp'=2,'seq'=8,'head'=2] {'seq'}, dimensions={1} | all-to-all | bytes 1048576 | tf_op jit(solution)/shard_map/all_to_all | solution.py:109
  36.3 25.3 %all_to_all.116 = bf16[8,256,128]{2,1,0:T(8,128)(2,1)S(1)} all-to-all(bf16[8,256,128]{2,1,0:T(8,128)(2,1)S(1)} %bitcast.582), channel_id=1, replica_groups=mesh['dp'=2,'seq'=8,'head'=2] {'seq'}, dimensions={0} | all-to-all | bytes 1048576 | tf_op jit(solution)/shard_map/all_to_all | solution.py:119
  64.6 11.1 %all-to-all-start.1 = ((bf16[128,8,256]{0,2,1:T(8,128)(2,1)}), bf16[128,8,256]{0,2,1:T(8,128)(2,1)S(1)}, u32[]{:S(2)}, u32[]{:S(2)}) async-start(bf16[128,8,256]{0,2,1:T(8,128)(2,1)} %bitcast.42), calls=%async_computation.1 | async-start | bytes 1048576 | tf_op jit(solution)/shard_map/all_to_all | solution.py:109
  77.5 38.6 %all_gather.47 = bf16[2048,32]{0,1:T(8,128)(2,1)S(1)} all-gather(bf16[128,32]{0,1:T(8,128)(2,1)S(1)} %copy-done.97), channel_id=1, replica_groups=mesh['dp'=2,'seq'=8,'head'=2] {'dp','seq'}, dimensions={0}, use_global_device_ids=true | all-gather | bytes 139264 | tf_op jit(solution)/shard_map/all_gather | solution.py:115
  120.1 5.6 fusion.19
  126.4 47.6 %fusion.184 = f32[2,8,128,4]{3,1,2,0:T(8,128)S(1)} fusion(f32[2,8,128,4]{3,1,2,0:T(8,128)S(1)} %copy.524), kind=kOutput, calls=%fused_computation.362 | output fusion | flops 1040384 | bytes 65536 | tf_op jit(solution)/shard_map/jvp(jit(cumsum))/reduce_window_sum | solution.py:39
  174.8 6.1 convolution_convert_fusion.6
  182.6 4.1 all-gather.15.cloned.1.call-done
  186.8 6.0 convolution_convert_fusion.5
  193.1 18.6 %all-gather.21.cloned.1.call-done = bf16[256,2048]{0,1:T(8,128)(2,1)} async-done(((bf16[256,1024]{0,1:T(8,128)(2,1)}), bf16[256,2048]{0,1:T(8,128)(2,1)}) %all-gather.21.cloned.1.call-update) | async-done | bytes 1048592 | tf_op jit(solution)/shard_map/all_gather | solution.py:118
  211.8 76.2 %all-gather.19.cloned.1.call-done = bf16[2048,2048]{1,0:T(8,128)(2,1)} async-done(((bf16[128,2048]{1,0:T(8,128)(2,1)}), bf16[2048,2048]{1,0:T(8,128)(2,1)}) %all-gather.19.cloned.1.call-update) | async-done | bytes 8388624 | tf_op jit(solution)/shard_map/all_gather | solution.py:121
  288.0 7.3 fusion.188
  295.2 3.0 copy.565
  298.4 12.4 %all-gather.17.cloned.1.call-done = bf16[2048,256]{1,0:T(8,128)(2,1)} async-done(((bf16[1024,256]{1,0:T(8,128)(2,1)}), bf16[2048,256]{1,0:T(8,128)(2,1)}) %all-gather.17.cloned.1.call-update) | async-done | bytes 1048592 | tf_op jit(solution)/shard_map/all_gather | solution.py:108
  310.8 6.0 convolution_convert_fusion.4
  319.3 2.9 copy.560
  322.2 6.9 fusion.44
  329.1 5.1 reshape.593
  334.2 5.2 copy.522
  339.5 2.6 fusion.43
  357.8 10.5 multiply_reduce_fusion.16
  368.3 3.1 copy.559
  371.4 2.6 multiply_reduce_fusion.15
  374.0 50.2 %psum.77 = f32[2,2,1024]{2,1,0:T(2,128)S(1)} all-reduce(f32[2,2,1024]{2,1,0:T(2,128)S(1)} %pad_maximum_fusion), channel_id=1, replica_groups=mesh['dp'=2,'seq'=8,'head'=2] {'seq','head'}, use_global_device_ids=true, to_apply=%region_4.5 | all-reduce | flops 4096 | bytes 32768 | tf_op jit(solution)/shard_map/psum | solution.py:144
  425.5 5.9 multiply_reduce_fusion.13
  431.5 3.6 fusion.72
  438.7 4.5 fusion.69
  443.2 3.5 fusion.111
  450.0 4.5 fusion.78
  454.5 3.2 fusion.51
  457.7 12.5 %fusion.12 = (f32[2,8,128,128]{3,2,1,0:T(8,128)}, f32[2,8,128,128,4]{3,2,4,1,0:T(8,128)}) fusion(f32[2,8,128,4]{2,3,1,0:T(4,128)S(1)} %copy-done.72, pred[2,8,128,128]{3,2,1,0:T(8,128)(4,1)S(1)} %copy-done.51, pred[8,128,128]{2,1,0:T(8,128)(4,1)S(1)} %copy-done.56, f32[2,8,128,128]{3,2,1,0:T(8,128)S(1)} %copy-done.41, ...), kind=kOutput, calls=%fused_computation.18 | convolution fusion | flops 824442880 | bytes 10944512 | tf_op jit(solution)/shard_map/transpose(jvp(sktuh,skuhp->skthp))/dot_general | solution.py:65
  470.2 4.6 fusion.90
  477.0 4.1 fusion.175
  481.2 9.8 multiply_reduce_fusion
  494.4 47.3 %fusion.185 = f32[2,8,128,4]{3,1,2,0:T(8,128)S(1)} fusion(f32[2,8,128,4]{3,1,2,0:T(8,128)S(1)} %copy.609), kind=kOutput, calls=%fused_computation.363 | output fusion | flops 1040384 | bytes 65536 | tf_op jit(solution)/shard_map/transpose(jvp(jit(cumsum)))/reduce_window_sum | solution.py:39
  542.3 4.8 copy.658
  547.1 5.6 reshape.594
  552.7 3.4 multiply_reduce_fusion.10
  568.4 8.1 fusion.156
  576.5 3.4 multiply_reduce_fusion.2
  580.0 8.5 fusion.189
  588.5 15.9 %add_convert_fusion = bf16[2048,2048]{1,0:T(8,128)(2,1)} fusion(f32[2048,2048]{1,0:T(8,128)} %fusion.156, f32[2048,2048]{1,0:T(8,128)} %fusion.189, bf16[2048,256]{1,0:T(8,128)(2,1)S(1)} %bitcast.562, bf16[2048,256]{1,0:T(8,128)(2,1)S(1)} %copy-done.36), kind=kOutput, calls=%fused_computation | convolution fusion | flops 2160066560 | bytes 44040192 | tf_op jit(solution)/shard_map/rc,kc->rk/dot_general | solution.py:166
  605.9 5.6 convolution_convert_fusion
  611.6 6.9 fusion.190
  618.8 6.9 convolution_convert_fusion.3
  625.7 6.9 convolution_convert_fusion.2
  632.7 6.9 convolution_convert_fusion.1
  639.7 2.8 fusion.150
  642.6 102.7 %reduce-scatter.13.cloned.1.call-done = bf16[128,2048]{1,0:T(8,128)(2,1)} async-done(((bf16[2048,2048]{1,0:T(8,128)(2,1)}), bf16[128,2048]{1,0:T(8,128)(2,1)}) %reduce-scatter.13.cloned.1.call-update) | async-done | bytes 524304 | tf_op jit(solution)/shard_map/reduce_scatter | solution.py:172
  747.3 107.0 %reduce-scatter.11.cloned.1.call-done = bf16[128,2048]{1,0:T(8,128)(2,1)} async-done(((bf16[2048,2048]{1,0:T(8,128)(2,1)}), bf16[128,2048]{1,0:T(8,128)(2,1)}) %reduce-scatter.11.cloned.1.call-update) | async-done | bytes 524304 | tf_op jit(solution)/shard_map/reduce_scatter | solution.py:150
  856.9 20.4 %reduce-scatter.25.cloned.1.call-done = f32[1024,4]{1,0:T(8,128)} async-done(((f32[2048,4]{1,0:T(8,128)}), f32[1024,4]{1,0:T(8,128)}) %reduce-scatter.25.cloned.1.call-update) | async-done | bytes 16400
  878.5 7.9 all_to_all.117
  886.5 14.0 %reduce-scatter.17.cloned.1.call-done = bf16[1024,256]{1,0:T(8,128)(2,1)} async-done(((bf16[2048,256]{1,0:T(8,128)(2,1)}), bf16[1024,256]{1,0:T(8,128)(2,1)}) %reduce-scatter.17.cloned.1.call-update) | async-done | bytes 524304 | tf_op jit(solution)/shard_map/reduce_scatter | solution.py:181
  900.5 5.5 all-to-all-start.3
  906.5 17.1 %reduce-scatter.19.cloned.1.call-done = bf16[1024,256]{1,0:T(8,128)(2,1)} async-done(((bf16[2048,256]{1,0:T(8,128)(2,1)}), bf16[1024,256]{1,0:T(8,128)(2,1)}) %reduce-scatter.19.cloned.1.call-update) | async-done | bytes 524304 | tf_op jit(solution)/shard_map/reduce_scatter | solution.py:181
  923.6 5.5 all-to-all-start.4
  930.5 15.7 %reduce-scatter.21.cloned.1.call-done = bf16[256,1024]{1,0:T(8,128)(2,1)} async-done(((bf16[256,2048]{1,0:T(8,128)(2,1)}), bf16[256,1024]{1,0:T(8,128)(2,1)}) %reduce-scatter.21.cloned.1.call-update) | async-done | bytes 524304 | tf_op jit(solution)/shard_map/reduce_scatter | solution.py:194
  948.1 5.5 all-to-all-start.6
  953.7 4.2 all-reduce.54
  957.9 19.1 %all-gather = f32[8,1,256]{2,1,0:T(1,128)S(1)} all-gather(f32[1,1,256]{2,1,0:T(1,128)S(1)} %bitcast.633), channel_id=1, replica_groups=mesh['dp'=2,'seq'=8,'head'=2] {'seq'}, dimensions={0}, use_global_device_ids=true | all-gather | bytes 9216 | tf_op jit(solution)/shard_map/all_gather | solution.py:202
  977.0 10.0 all-gather.1
  987.0 25.6 %all_gather.54 = f32[4,2048]{1,0:T(4,128)S(1)} all-gather(f32[4,256]{1,0:T(4,128)S(1)} %get-tuple-element.164), channel_id=1, replica_groups=mesh['dp'=2,'seq'=8,'head'=2] {'seq'}, dimensions={1}, use_global_device_ids=true | all-gather | bytes 36864 | tf_op jit(solution)/shard_map/all_gather | solution.py:202
  1013.2 16.6 %all-reduce.53 = (f32[32]{0:T(128)}, f32[32]{0:T(128)}, f32[32]{0:T(128)}) all-reduce(f32[32]{0:T(128)S(1)} %dynamic-update-slice, f32[32]{0:T(128)S(1)} %dynamic-update-slice.1, f32[32]{0:T(128)S(1)} %dynamic-update-slice.2), channel_id=1, replica_groups=mesh['dp'=2,'seq'=8,'head'=2] {'seq'}, use_global_device_ids=true, to_apply=%add.49 | all-reduce | flops 96 | bytes 768
  1033.3 56.5 %all-reduce.52 = (f32[2048]{0:T(1024)}, f32[4,256]{1,0:T(4,128)}, f32[256]{0:T(256)}) all-reduce(f32[2048]{0:T(1024)S(1)} %get-tuple-element.135, f32[4,256]{1,0:T(4,128)S(1)} %pad_add_fusion.10, f32[256]{0:T(256)S(1)} %get-tuple-element.131), channel_id=1, replica_groups=mesh['dp'=2,'seq'=8,'head'=2] {'dp','seq','head'}, use_global_device_ids=true, to_apply=%region_33.34 | all-reduce | flops 3328 | bytes 26624 | tf_op jit(solution)/shard_map/psum | solution.py:203
  (405 shorter events, 85.3 us)
Async XLA Ops:
  7.2 112.9 %all-gather.11.cloned.1.call-start = ((), (), s32[]{:S(2)}) async-start(), calls=%async_computation.15 | async-start | bytes 8912896 | tf_op jit(solution)/shard_map/all_gather | solution.py:105
  11.7 24.6 %copy-start.47 = (bf16[2048,128]{1,0:T(8,128)(2,1)S(1)}, bf16[2048,128]{1,0:T(8,128)(2,1)}, u32[]{:S(2)}) copy-start(bf16[2048,128]{1,0:T(8,128)(2,1)} %param.31) | copy-start | bytes 1572868
  11.7 163.1 %all-gather.13.cloned.1.call-start = ((), (), s32[]{:S(2)}) async-start(), calls=%async_computation.16 | async-start | bytes 1572864 | tf_op jit(solution)/shard_map/all_gather | solution.py:108
  34.5 28.3 %copy-start.43 = (bf16[2,1,128,2048]{3,2,1,0:T(8,128)(2,1)S(1)}, bf16[2,1,128,2048]{3,2,1,0:T(8,128)(2,1)}, u32[]{:S(2)}) copy-start(bf16[2,1,128,2048]{3,2,1,0:T(8,128)(2,1)} %param.33) | copy-start | bytes 3145732
  35.5 151.3 %all-gather.15.cloned.1.call-start = ((), (), s32[]{:S(2)}) async-start(), calls=%async_computation.17 | async-start | bytes 1114112 | tf_op jit(solution)/shard_map/all_gather | solution.py:117
  36.2 175.5 %all-gather.21.cloned.1.call-start = ((), (), s32[]{:S(2)}) async-start(), calls=%async_computation.20 | async-start | bytes 1572864 | tf_op jit(solution)/shard_map/all_gather | solution.py:118
  36.3 27.3 %copy-start.48 = (bf16[128,2048]{1,0:T(8,128)(2,1)S(1)}, bf16[128,2048]{1,0:T(8,128)(2,1)}, u32[]{:S(2)}) copy-start(bf16[128,2048]{1,0:T(8,128)(2,1)} %param.19) | copy-start | bytes 1572868
  62.6 13.1 %copy-start.106 = (f32[32]{0:T(128)S(1)}, f32[32]{0:T(128)}, u32[]{:S(2)}) copy-start(f32[32]{0:T(128)} %param.28) | copy-start | bytes 388
  62.6 14.8 %copy-start.97 = (bf16[128,32]{0,1:T(8,128)(2,1)S(1)}, bf16[128,32]{0,1:T(8,128)(2,1)}, u32[]{:S(2)}) copy-start(bf16[128,32]{0,1:T(8,128)(2,1)} %param.22) | copy-start | bytes 24580
  62.6 53.5 %copy-start.112 = (f32[32]{0:T(128)S(1)}, f32[32]{0:T(128)}, u32[]{:S(2)}) copy-start(f32[32]{0:T(128)} %param.27) | copy-start | bytes 388
  62.7 53.5 %copy-start.113 = (f32[32]{0:T(128)S(1)}, f32[32]{0:T(128)}, u32[]{:S(2)}) copy-start(f32[32]{0:T(128)} %param.29) | copy-start | bytes 388
  62.7 55.8 %copy-start.108 = (s32[2,1]{0,1:T(1,128)S(1)}, s32[2,1]{0,1:T(1,128)}, u32[]{:S(2)}) copy-start(s32[2,1]{0,1:T(1,128)} %param.32) | copy-start | bytes 28
  62.7 55.9 %copy-start.104 = (f32[4,256]{1,0:T(4,128)S(1)}, f32[4,256]{1,0:T(4,128)}, u32[]{:S(2)}) copy-start(f32[4,256]{1,0:T(4,128)} %param.25) | copy-start | bytes 12292
  62.7 225.3 %all-gather.19.cloned.1.call-start = ((), (), s32[]{:S(2)}) async-start(), calls=%async_computation.19 | async-start | bytes 8912896 | tf_op jit(solution)/shard_map/all_gather | solution.py:121
  64.6 54.4 %all-to-all-start.1 = ((bf16[128,8,256]{0,2,1:T(8,128)(2,1)}), bf16[128,8,256]{0,2,1:T(8,128)(2,1)S(1)}, u32[]{:S(2)}, u32[]{:S(2)}) async-start(bf16[128,8,256]{0,2,1:T(8,128)(2,1)} %bitcast.42), calls=%async_computation.1 | async-start | bytes 1048576 | tf_op jit(solution)/shard_map/all_to_all | solution.py:109
  75.7 235.2 %all-gather.17.cloned.1.call-start = ((), (), s32[]{:S(2)}) async-start(), calls=%async_computation.18 | async-start | bytes 1572864 | tf_op jit(solution)/shard_map/all_gather | solution.py:108
  75.8 50.1 %copy-start.100 = (f32[4]{0:T(128)}, f32[4]{0:T(128)S(1)}, u32[]{:S(2)}) copy-start(f32[4]{0:T(128)S(1)} %fusion.174) | copy-start | bytes 52
  76.7 245.5 %copy-start.81 = (f32[1,256]{1,0:T(1,128)}, f32[1,256]{1,0:T(1,128)S(1)}, u32[]{:S(2)}) copy-start(f32[1,256]{1,0:T(1,128)S(1)} %get-tuple-element.230) | copy-start | bytes 3076
  76.7 245.5 %copy-start.83 = (f32[1,256]{1,0:T(1,128)}, f32[1,256]{1,0:T(1,128)S(1)}, u32[]{:S(2)}) copy-start(f32[1,256]{1,0:T(1,128)S(1)} %get-tuple-element.231) | copy-start | bytes 3076
  76.7 245.5 %copy-start.85 = (f32[1,256]{1,0:T(1,128)}, f32[1,256]{1,0:T(1,128)S(1)}, u32[]{:S(2)}) copy-start(f32[1,256]{1,0:T(1,128)S(1)} %get-tuple-element.232) | copy-start | bytes 3076
  76.7 245.5 %copy-start.87 = (f32[1,256]{1,0:T(1,128)}, f32[1,256]{1,0:T(1,128)S(1)}, u32[]{:S(2)}) copy-start(f32[1,256]{1,0:T(1,128)S(1)} %get-tuple-element.233) | copy-start | bytes 3076
  116.3 241.5 %copy-start.115 = (f32[4]{0:T(128)}, f32[4]{0:T(128)S(1)}, u32[]{:S(2)}) copy-start(f32[4]{0:T(128)S(1)} %dynamic_slice.33) | copy-start | bytes 52
  118.5 74.2 %copy-start.67 = (pred[2,8,128]{2,1,0:T(8,128)(4,1)}, pred[2,8,128]{2,1,0:T(8,128)(4,1)S(1)}, u32[]{:S(2)}) copy-start(pred[2,8,128]{2,1,0:T(8,128)(4,1)S(1)} %broadcast_compare_fusion.2) | copy-start | bytes 6148
  118.6 220.8 %copy-start.89 = (f32[1,256]{1,0:T(1,128)}, f32[1,256]{1,0:T(1,128)S(1)}, u32[]{:S(2)}) copy-start(f32[1,256]{1,0:T(1,128)S(1)} %get-tuple-element.239) | copy-start | bytes 3076
  118.6 220.8 %copy-start.91 = (f32[1,256]{1,0:T(1,128)}, f32[1,256]{1,0:T(1,128)S(1)}, u32[]{:S(2)}) copy-start(f32[1,256]{1,0:T(1,128)S(1)} %get-tuple-element.240) | copy-start | bytes 3076
  118.6 220.8 %copy-start.93 = (f32[1,256]{1,0:T(1,128)}, f32[1,256]{1,0:T(1,128)S(1)}, u32[]{:S(2)}) copy-start(f32[1,256]{1,0:T(1,128)S(1)} %get-tuple-element.241) | copy-start | bytes 3076
  118.6 220.8 %copy-start.95 = (f32[1,256]{1,0:T(1,128)}, f32[1,256]{1,0:T(1,128)S(1)}, u32[]{:S(2)}) copy-start(f32[1,256]{1,0:T(1,128)S(1)} %get-tuple-element.242) | copy-start | bytes 3076
  118.8 238.9 %copy-start.55 = (pred[8,128,128]{2,1,0:T(8,128)(4,1)}, pred[8,128,128]{2,1,0:T(8,128)(4,1)S(1)}, u32[]{:S(2)}) copy-start(pred[8,128,128]{2,1,0:T(8,128)(4,1)S(1)} %get-tuple-element.237) | copy-start | bytes 393220
  119.0 238.7 %copy-start.50 = (pred[2,8,128,128]{3,2,1,0:T(8,128)(4,1)}, pred[2,8,128,128]{3,2,1,0:T(8,128)(4,1)S(1)}, u32[]{:S(2)}) copy-start(pred[2,8,128,128]{3,2,1,0:T(8,128)(4,1)S(1)} %broadcast_and_fusion) | copy-start | bytes 786436
  120.1 519.6 %reduce-scatter.15.cloned.1.call-start = ((), (), s32[]{:S(2)}) async-start(), calls=%async_computation.24 | async-start | bytes 2228224 | tf_op jit(solution)/shard_map/reduce_scatter | solution.py:163
  174.7 183.0 %copy-start.71 = (f32[2,8,128,4]{2,3,1,0:T(4,128)}, f32[2,8,128,4]{2,3,1,0:T(4,128)S(1)}, u32[]{:S(2)}) copy-start(f32[2,8,128,4]{2,3,1,0:T(4,128)S(1)} %copy.525) | copy-start | bytes 98308
  192.9 154.8 %copy-start.59 = (f32[2,8,128,4]{2,3,1,0:T(4,128)}, f32[2,8,128,4]{2,3,1,0:T(4,128)S(1)}, u32[]{:S(2)}) copy-start(f32[2,8,128,4]{2,3,1,0:T(4,128)S(1)} %copy.546) | copy-start | bytes 98308
  193.1 146.3 %copy-start = (f32[8,2,128,256]{3,2,0,1:T(8,128)}, f32[8,2,128,256]{3,2,0,1:T(8,128)S(1)}, u32[]{:S(2)}) copy-start(f32[8,2,128,256]{3,2,0,1:T(8,128)S(1)} %copy.523) | copy-start | bytes 6291460
  298.4 48.0 %copy-start.76 = (f32[2,4]{1,0:T(2,128)}, f32[2,4]{1,0:T(2,128)S(1)}, u32[]{:S(2)}) copy-start(f32[2,4]{1,0:T(2,128)S(1)} %get-tuple-element.150) | copy-start | bytes 100
  298.4 51.5 %copy-start.63 = (f32[2,4]{1,0:T(2,128)}, f32[2,4]{1,0:T(2,128)S(1)}, u32[]{:S(2)}) copy-start(f32[2,4]{1,0:T(2,128)S(1)} %get-tuple-element.154) | copy-start | bytes 100
  298.4 51.5 %copy-start.65 = (f32[2,4]{1,0:T(2,128)}, f32[2,4]{1,0:T(2,128)S(1)}, u32[]{:S(2)}) copy-start(f32[2,4]{1,0:T(2,128)S(1)} %get-tuple-element.157) | copy-start | bytes 100
  298.4 52.0 %copy-start.74 = (f32[2,4]{1,0:T(2,128)}, f32[2,4]{1,0:T(2,128)S(1)}, u32[]{:S(2)}) copy-start(f32[2,4]{1,0:T(2,128)S(1)} %get-tuple-element.151) | copy-start | bytes 100
  342.2 13.2 %copy-start.3 = (f32[2,1024,128]{2,1,0:T(8,128)}, f32[2,1024,128]{2,1,0:T(8,128)S(1)}, u32[]{:S(2)}) copy-start(f32[2,1024,128]{2,1,0:T(8,128)S(1)} %get-tuple-element.221) | copy-start | bytes 3145732
  355.4 12.9 %copy-start.27 = (f32[2,8,128,4,64]{2,4,3,1,0:T(8,128)}, f32[2,8,128,4,64]{2,4,3,1,0:T(8,128)S(1)}, u32[]{:S(2)}) copy-start(f32[2,8,128,4,64]{2,4,3,1,0:T(8,128)S(1)} %fusion.55) | copy-start | bytes 6291460
  494.0 48.1 %copy-start.53 = (f32[2,8,128,4]{2,3,1,0:T(4,128)S(1)}, f32[2,8,128,4]{2,3,1,0:T(4,128)}, u32[]{:S(2)}) copy-start(f32[2,8,128,4]{2,3,1,0:T(4,128)} %get-tuple-element.137) | copy-start | bytes 98308
  494.0 48.1 %copy-start.101 = (f32[4]{0:T(128)S(1)}, f32[4]{0:T(128)}, u32[]{:S(2)}) copy-start(f32[4]{0:T(128)} %copy-done.100) | copy-start | bytes 52
  494.0 48.1 %copy-start.103 = (f32[4]{0:T(128)S(1)}, f32[4]{0:T(128)}, u32[]{:S(2)}) copy-start(f32[4]{0:T(128)} %copy-done.102) | copy-start | bytes 52
  568.3 176.9 %reduce-scatter.13.cloned.1.call-start = ((), (), s32[]{:S(2)}) async-start(), calls=%async_computation.23 | async-start | bytes 8912896 | tf_op jit(solution)/shard_map/reduce_scatter | solution.py:172
  604.4 249.9 %reduce-scatter.11.cloned.1.call-start = ((), (), s32[]{:S(2)}) async-start(), calls=%async_computation.21 | async-start | bytes 8912896 | tf_op jit(solution)/shard_map/reduce_scatter | solution.py:150
  611.6 265.8 %reduce-scatter.25.cloned.1.call-start = ((), (), s32[]{:S(2)}) async-start(), calls=%async_computation.31 | async-start | bytes 1572864
  618.6 281.9 %reduce-scatter.17.cloned.1.call-start = ((), (), s32[]{:S(2)}) async-start(), calls=%async_computation.26 | async-start | bytes 1572864 | tf_op jit(solution)/shard_map/reduce_scatter | solution.py:181
  625.7 297.9 %reduce-scatter.19.cloned.1.call-start = ((), (), s32[]{:S(2)}) async-start(), calls=%async_computation.27 | async-start | bytes 1572864 | tf_op jit(solution)/shard_map/reduce_scatter | solution.py:181
  632.6 313.6 %reduce-scatter.21.cloned.1.call-start = ((), (), s32[]{:S(2)}) async-start(), calls=%async_computation.28 | async-start | bytes 1572864 | tf_op jit(solution)/shard_map/reduce_scatter | solution.py:194
  639.6 105.7 %copy-start.31 = (bf16[2,1,128,2048]{3,2,1,0:T(8,128)(2,1)S(1)}, bf16[2,1,128,2048]{3,2,1,0:T(8,128)(2,1)}, u32[]{:S(2)}) copy-start(bf16[2,1,128,2048]{3,2,1,0:T(8,128)(2,1)} %param.17) | copy-start | bytes 3145732
  639.6 105.7 %copy-start.62 = (f32[2048]{0:T(1024)S(1)}, f32[2048]{0:T(1024)}, u32[]{:S(2)}) copy-start(f32[2048]{0:T(1024)} %param.18) | copy-start | bytes 24580
  639.6 105.7 %copy-start.99 = (f32[128]{0:T(128)S(1)}, f32[128]{0:T(128)}, u32[]{:S(2)}) copy-start(f32[128]{0:T(128)} %copy-done.98) | copy-start | bytes 1540
  639.6 390.3 %reduce-scatter.23.cloned.1.call-start = ((), (), s32[]{:S(2)}) async-start(), calls=%async_computation.29 | async-start | bytes 2228224 | tf_op jit(solution)/shard_map/reduce_scatter | solution.py:190
  639.7 105.6 %copy-start.49 = (f32[128,256]{1,0:T(8,128)S(1)}, f32[128,256]{1,0:T(8,128)}, u32[]{:S(2)}) copy-start(f32[128,256]{1,0:T(8,128)} %reduce-scatter.15.cloned.1.call-done) | copy-start | bytes 393220
  642.5 104.8 %copy-start.111 = (f32[128]{0:T(128)S(1)}, f32[128]{0:T(128)}, u32[]{:S(2)}) copy-start(f32[128]{0:T(128)} %copy-done.110) | copy-start | bytes 1540
  642.5 211.8 %copy-start.44 = (bf16[2,1,128,2048]{3,2,1,0:T(8,128)(2,1)S(1)}, bf16[2,1,128,2048]{3,2,1,0:T(8,128)(2,1)}, u32[]{:S(2)}) copy-start(bf16[2,1,128,2048]{3,2,1,0:T(8,128)(2,1)} %param.33) | copy-start | bytes 3145732
  642.5 447.2 %all-gather.23.cloned.1.call-start = ((), (), s32[]{:S(2)}) async-start(), calls=%async_computation.22 | async-start | bytes 1572864 | tf_op jit(solution)/shard_map/all_gather | solution.py:199
  856.9 72.2 %copy-start.114 = (u32[32]{0:T(128)S(1)}, u32[32]{0:T(128)}, u32[]{:S(2)}) copy-start(u32[32]{0:T(128)} %constant.176) | copy-start | bytes 388
  900.5 23.1 %all-to-all-start.3 = ((bf16[8,128,256]{2,1,0:T(8,128)(2,1)}), bf16[8,128,256]{2,1,0:T(8,128)(2,1)S(1)}, u32[]{:S(2)}, u32[]{:S(2)}) async-start(bf16[8,128,256]{2,1,0:T(8,128)(2,1)} %bitcast.584), calls=%async_computation.7 | async-start | bytes 1048576 | tf_op jit(solution)/shard_map/all_to_all | solution.py:180
  905.9 183.8 %all-gather.25.cloned.1.call-start = ((), (), s32[]{:S(2)}) async-start(), calls=%async_computation.25 | async-start | bytes 3145728 | tf_op jit(solution)/shard_map/all_gather | solution.py:199
  906.0 47.7 %copy-start.107 = (f32[32]{0:T(128)S(1)}, f32[32]{0:T(128)}, u32[]{:S(2)}) copy-start(f32[32]{0:T(128)} %param.28) | copy-start | bytes 388
  906.0 47.7 %copy-start.109 = (f32[4]{0:T(128)S(1)}, f32[4]{0:T(128)}, u32[]{:S(2)}) copy-start(f32[4]{0:T(128)} %get-tuple-element.130) | copy-start | bytes 52
  923.6 24.5 %all-to-all-start.4 = ((bf16[8,128,256]{2,1,0:T(8,128)(2,1)}), bf16[8,128,256]{2,1,0:T(8,128)(2,1)S(1)}, u32[]{:S(2)}, u32[]{:S(2)}) async-start(bf16[8,128,256]{2,1,0:T(8,128)(2,1)} %bitcast.583), calls=%async_computation.9 | async-start | bytes 1048576 | tf_op jit(solution)/shard_map/all_to_all | solution.py:180
  948.1 84.1 %all-to-all-start.6 = ((bf16[256,8,128]{2,0,1:T(8,128)(2,1)}), bf16[256,8,128]{2,0,1:T(8,128)(2,1)S(1)}, u32[]{:S(2)}, u32[]{:S(2)}) async-start(bf16[256,8,128]{2,0,1:T(8,128)(2,1)} %copy_bitcast_fusion), calls=%async_computation.12 | async-start | bytes 1048576 | tf_op jit(solution)/shard_map/all_to_all | solution.py:193
  953.6 136.2 %all-reduce.57.cloned.1.call-start = ((), (), s32[]{:S(2)}) async-start(), calls=%async_computation.30 | async-start | bytes 262144 | tf_op jit(solution)/shard_map/psum | solution.py:191
  (74 other events, 296.7 us)
Sparse Core Ops, SparseCore 0:
  11.8 92.4 all-gather.10
  106.4 24.8 all-gather.12
  134.0 52.7 all-gather.14
  188.8 22.9 all-gather.20
  214.3 73.5 all-gather.18
  289.9 20.8 all-gather.16
  568.4 66.2 reduce-scatter.14
  639.3 105.9 reduce-scatter.12
  749.9 104.3 reduce-scatter.10
  857.1 20.2 reduce-scatter.24
  880.1 20.3 reduce-scatter.16
  903.3 20.3 reduce-scatter.18
  925.8 20.3 reduce-scatter.20
  949.0 68.5 reduce-scatter.22
  1019.1 21.8 all-gather.22
  1043.1 11.7 all-gather.24
  1057.1 19.0 all-reduce.56

commit v2 on v1

v2 whole, which is shorter than its diff:
```python
import functools
import jax
import jax.numpy as jnp
from jax import lax
from jax.experimental import pallas as pl
from jax.experimental.pallas import tpu as pltpu

from jax.sharding import PartitionSpec as P

EPSILON = 1e-05
BF16 = jnp.bfloat16
F32 = jnp.float32
NN = (((1,), (0,)), ((), ()))
NT = (((1,), (1,)), ((), ()))
TN = (((0,), (0,)), ((), ()))


def mm(a, b, dims=NN):
    return lax.dot_general(a.astype(BF16), b.astype(BF16), dims, preferred_element_type=F32)


def pieces(a, count):
    out = []
    for _ in range(count):
        top = a.astype(BF16)
        out.append(top)
        a = a - top.astype(F32)
    return out


def mm_left(exact, a, count, dims=NN):
    return sum(mm(exact, piece, dims) for piece in pieces(a, count))


def mm_right(a, exact, count, dims=NN):
    return sum(mm(piece, exact, dims) for piece in pieces(a, count))


def sigmoid(x):
    return 1.0 / (1.0 + jnp.exp(-x))


def window(cur, before):
    return jnp.concatenate([before, cur], axis=0)


def column_sum(x):
    return jnp.sum(x, axis=0, keepdims=True)


def iota(shape, axis):
    return lax.broadcasted_iota(jnp.int32, shape, axis)


def one_hot(cond):
    return jnp.where(cond, 1.0, 0.0).astype(BF16)


def conv_window(p_ref, k, lo, hi):
    span = p_ref.shape[2]
    cur = p_ref[k, 0, :, lo:hi].astype(F32)
    prev = p_ref[jnp.maximum(k - 1, 0), 0, span - 16 :, lo:hi].astype(F32)[8:]
    return window(cur, jnp.where(k > 0, prev, 0.0))


def taps(win, span, j):
    return win[5 + j : 5 + j + span]


def conv(win, span, w_ref, b_ref):
    acc = b_ref[...] + w_ref[3:4, :] * taps(win, span, 3)
    for j in range(3):
        acc = acc + w_ref[j : j + 1, :] * taps(win, span, j)
    return acc


def chunk_masks(span, k, prefix):
    t, s = iota((span, span), 0), iota((span, span), 1)
    return t, s, (s <= t) | (s + k * span < prefix)


def forward_kernel(
    heads, state, prefix_ref, p_ref, gs_ref, cxw, cxb, cbw, cbb, dtb, nega, dsk, gain,
    xc_ref, bcc_ref, dt_ref, cum_ref, mixed_ref, sin_ref, rin_ref, sums_ref, s_scr, r_scr,
):
    count, _, span, _ = p_ref.shape
    width = cxw.shape[1]
    head_width = width // heads
    prefix = prefix_ref[pl.program_id(0)]
    expand = one_hot(iota((128, width), 0) == iota((128, width), 1) // head_width)
    tri = one_hot(iota((span, span), 1) <= iota((span, span), 0))
    row = iota((span, 1), 0)

    s_scr[...] = jnp.zeros_like(s_scr)
    r_scr[...] = jnp.zeros_like(r_scr)

    def ascend(k, carry):
        xc = conv(conv_window(p_ref, k, width, 2 * width), span, cxw, cxb)
        bcc = conv(conv_window(p_ref, k, 2 * width, 2 * width + 2 * state), span, cbw, cbb)
        xc_ref[k, 0] = xc
        bcc_ref[k, 0] = bcc
        v = xc * sigmoid(xc)
        raw = mm(p_ref[k, 0, :, 2 * width + 2 * state :], expand) + dtb[...]
        dt = jnp.maximum(raw, 0.0) + jnp.log1p(jnp.exp(-jnp.abs(raw)))
        cum = mm_left(tri, dt * nega[...], 3)
        dt_ref[k, 0] = dt
        cum_ref[k, 0] = cum
        b = bcc[:, :state] * sigmoid(bcc[:, :state])
        end = cum[span - 1 :, :]
        state_in = s_scr[...]
        sin_ref[k, 0] = state_in
        s_scr[...] = jnp.exp(end) * state_in + mm(b, jnp.exp(end - cum) * (dt * v), TN)
        return carry

    lax.fori_loop(0, count, ascend, 0)

    def descend(step, carry):
        k = count - 1 - step
        xc, bcc = xc_ref[k, 0], bcc_ref[k, 0]
        dt, cum = dt_ref[k, 0], cum_ref[k, 0]
        v = xc * sigmoid(xc)
        bc = bcc * sigmoid(bcc)
        b, c = bc[:, :state].astype(BF16), bc[:, state:].astype(BF16)
        end = cum[span - 1 :, :]
        w = dt * v
        t, s, mask = chunk_masks(span, k, prefix)
        scores = jnp.where(mask, mm(c, b, NT), 0.0)
        cum_t = cum.T
        lane_head = iota((span, width), 1) // head_width
        wb = w.astype(BF16)
        y = dsk[...] * v
        for h in range(heads):
            at = h * head_width
            decay = jnp.exp(-jnp.abs(cum[:, at : at + 1] - cum_t[at : at + 1, :]))
            y = y + jnp.where(lane_head == h, mm(scores * decay, wb), 0.0)
        back = r_scr[...]
        rin_ref[k, 0] = back
        y = y + jnp.exp(cum) * mm(c, sin_ref[k, 0]) + jnp.exp(end - cum) * mm(c, back)
        mixed_ref[k, 0] = y
        inside = row + k * span < prefix
        r_scr[...] = jnp.exp(end) * back + mm(b, jnp.where(inside, jnp.exp(cum) * w, 0.0), TN)
        gate = p_ref[k, 0, :, :width].astype(F32)
        gated = y * (gate * sigmoid(gate))
        ones = jnp.ones((8, width), BF16)
        square = mm_left(ones, gated * gated, 2, NT)
        cross = mm_left(ones, gated * (gs_ref[k, 0] * gain[...]), 2, NT)
        sums_ref[k, 0] = jnp.where(iota((8, span), 0) == 0, square, cross)
        return carry

    lax.fori_loop(0, count, descend, 0)


def backward_kernel(
    heads, state, full_inner, prefix_ref, p_ref, gs_ref, xc_ref, bcc_ref, dt_ref, cum_ref, mixed_ref, sin_ref,
    rin_ref, tot_ref, cxw, cxb, cbw, cbb, dtb, nega, dsk, gain,
    g_ref, scaled_ref, small_ref, smallbc_ref, dm_scr, j_scr, h_scr, nx_scr, nb_scr, jrun_scr,
):
    count, _, span, _ = p_ref.shape
    width = cxw.shape[1]
    head_width = width // heads
    prefix = prefix_ref[pl.program_id(0)]
    lane = iota((span, width), 1)
    lane_head = lane // head_width
    expand = one_hot(iota((128, width), 0) == iota((128, width), 1) // head_width)
    pick = one_hot(iota((width, 128), 0) == iota((width, 128), 1) * head_width)
    same_head = one_hot(iota((width, width), 0) // head_width == iota((width, width), 1) // head_width)
    later = one_hot(iota((span, span), 1) >= iota((span, span), 0))
    row = iota((span, 1), 0)

    @pl.when(pl.program_id(0) == 0)
    def _():
        small_ref[...] = jnp.zeros_like(small_ref)
        smallbc_ref[...] = jnp.zeros_like(smallbc_ref)

    for ref in (h_scr, nx_scr, nb_scr, jrun_scr):
        ref[...] = jnp.zeros_like(ref)

    def ascend(k, carry):
        tot = tot_ref[k, 0].T
        mean_sq = tot[:, 0:1] * (1.0 / full_inner)
        mean_x = tot[:, 1:2] * (1.0 / full_inner)
        scale = lax.rsqrt(mean_sq + EPSILON)
        gate = p_ref[k, 0, :, :width].astype(F32)
        sig = sigmoid(gate)
        act = gate * sig
        mixed = mixed_ref[k, 0]
        gated = mixed * act
        grad_scaled = gs_ref[k, 0]
        unit = gated * scale
        scaled_ref[k, 0] = (unit * gain[...]).astype(BF16)
        small_ref[5:6, :] += column_sum(grad_scaled * unit)
        dgated = grad_scaled * gain[...] * scale - unit * (scale * scale * mean_x)
        g_ref[k, 0, :, :width] = (dgated * mixed * (sig * (1.0 + gate * (1.0 - sig)))).astype(BF16)
        dm = dgated * act
        dm_scr[k] = dm
        cum = cum_ref[k, 0]
        end = cum[span - 1 :, :]
        cc = bcc_ref[k, 0, :, state:]
        c = cc * sigmoid(cc)
        jrun = jrun_scr[...]
        j_scr[k] = jrun
        jrun_scr[...] = jnp.exp(end) * jrun + mm(c, jnp.exp(end - cum) * dm, TN)
        return carry

    lax.fori_loop(0, count, ascend, 0)

    def descend(step, carry):
        k = count - 1 - step
        xc, bcc = xc_ref[k, 0], bcc_ref[k, 0]
        dt, cum, dm = dt_ref[k, 0], cum_ref[k, 0], dm_scr[k]
        xsig = sigmoid(xc)
        v = xc * xsig
        bsig = sigmoid(bcc)
        bc = bcc * bsig
        b, c = bc[:, :state].astype(BF16), bc[:, state:].astype(BF16)
        end = cum[span - 1 :, :]
        w = dt * v
        wb = w.astype(BF16)
        dmb = dm.astype(BF16)
        t, s, mask = chunk_masks(span, k, prefix)
        scores = jnp.where(mask, mm(c, b, NT), 0.0)
        side = jnp.where(t > s, 1.0, jnp.where(t < s, -1.0, 0.0))
        cum_t = cum.T
        dscore = jnp.zeros((span, span), F32)
        dw = jnp.zeros((span, width), F32)
        z = jnp.zeros((span, width), F32)
        for h in range(heads):
            at = h * head_width
            decay = jnp.exp(-jnp.abs(cum[:, at : at + 1] - cum_t[at : at + 1, :]))
            weight = scores * decay
            dm_h = jnp.where(lane_head == h, dmb, jnp.zeros_like(dmb))
            dweight = mm(dm_h, wb, NT)
            dw = dw + mm(weight, dm_h, TN)
            dscore = dscore + decay * dweight
            q = weight * dweight * side
            diff = jnp.sum(q - q.T, axis=1, keepdims=True)
            z = z + jnp.where(lane == at, diff, 0.0)
        dscore = jnp.where(mask, dscore, 0.0).astype(BF16)
        inside = row + k * span < prefix
        grow = jnp.exp(cum)
        fall = jnp.exp(end - cum)
        grow_in = jnp.where(inside, grow, 0.0)
        whole = jnp.exp(end)
        state_in, back_in = sin_ref[k, 0], rin_ref[k, 0]
        hgrad, jgrad = h_scr[...], j_scr[k]
        front = dm * grow
        rear = dm * fall
        wf = w * fall
        wg = w * grow_in
        bh, bj = mm(b, hgrad), mm(b, jgrad)
        out_b = rear * mm(c, back_in)
        src_f = wf * bh
        z = z + front * mm(c, state_in) - out_b - src_f + wg * bj
        edge = column_sum(out_b + src_f) + whole * column_sum(hgrad * state_in + jgrad * back_in)
        dw = dw + fall * bh + grow_in * bj
        dc = mm(dscore, b) + mm(front, state_in, NT) + mm(rear, back_in, NT)
        db = mm(dscore, c, TN) + mm(wf, hgrad, NT) + mm(wg, jgrad, NT)
        h_scr[...] = whole * hgrad + mm(c, front, TN)
        drate = mm_right(mm_left(later, z, 2) + edge, same_head, 2)
        raw = mm(p_ref[k, 0, :, 2 * width + 2 * state :], expand) + dtb[...]
        draw = (mm_right(v * dw, same_head, 2) + drate * nega[...]) * sigmoid(raw)
        small_ref[6:7, :] += column_sum(draw)
        small_ref[7:8, :] += column_sum(drate * (dt * nega[...]))
        small_ref[8:9, :] += column_sum(dm * v)
        g_ref[k, 0, :, 2 * width + 2 * state :] = mm(draw, pick).astype(BF16)
        dxc = (dt * dw + dsk[...] * dm) * (xsig * (1.0 + xc * (1.0 - xsig)))
        dbc = jnp.concatenate([db, dc], axis=1) * (bsig * (1.0 + bcc * (1.0 - bsig)))
        for grad, nref, sref, wref, lo, hi in (
            (dxc, nx_scr, small_ref, cxw, width, 2 * width),
            (dbc, nb_scr, smallbc_ref, cbw, 2 * width, 2 * width + 2 * state),
        ):
            win = conv_window(p_ref, k, lo, hi)
            for j in range(4):
                sref[j : j + 1, :] += column_sum(grad * taps(win, span, j))
            sref[4:5, :] += column_sum(grad)
            ext = jnp.concatenate([grad, nref[...]], axis=0)
            nref[...] = grad[:8]
            back = wref[3:4, :] * grad
            for j in range(3):
                back = back + wref[j : j + 1, :] * ext[3 - j : 3 - j + span]
            g_ref[k, 0, :, lo:hi] = back.astype(BF16)
        return carry

    lax.fori_loop(0, count, descend, 0)


def group_block(shape):
    return pl.BlockSpec((shape[0], 1) + tuple(shape[2:]), lambda g: (0, g, 0, 0))


def whole_block(a):
    return pl.BlockSpec(a.shape, lambda g: (0,) * a.ndim)


def ssd_forward(heads, state, prefix, p, gs, params):
    count, group, span, _ = p.shape
    width = params[0].shape[1]
    outs = [
        (count, group, span, width), (count, group, span, 2 * state), (count, group, span, width),
        (count, group, span, width), (count, group, span, width), (count, group, state, width),
        (count, group, state, width), (count, group, 8, span),
    ]
    return pl.pallas_call(
        functools.partial(forward_kernel, heads, state),
        grid=(group,),
        in_specs=[pl.BlockSpec(memory_space=pltpu.SMEM), group_block(p.shape), group_block(gs.shape)]
        + [whole_block(a) for a in params],
        out_specs=[group_block(o) for o in outs],
        out_shape=[jax.ShapeDtypeStruct(o, F32) for o in outs],
        scratch_shapes=[pltpu.VMEM((state, width), F32)] * 2,
        compiler_params=pltpu.CompilerParams(vmem_limit_bytes=56 << 20),
    )(prefix, p, gs, *params)


def ssd_backward(heads, state, full_inner, prefix, p, gs, saved, totals, params):
    count, group, span, cols = p.shape
    width = params[0].shape[1]
    ins = (p, gs) + tuple(saved) + (totals,)
    return pl.pallas_call(
        functools.partial(backward_kernel, heads, state, full_inner),
        grid=(group,),
        in_specs=[pl.BlockSpec(memory_space=pltpu.SMEM)]
        + [group_block(a.shape) for a in ins]
        + [whole_block(a) for a in params],
        out_specs=[
            group_block(p.shape), group_block((count, group, span, width)),
            pl.BlockSpec((16, width), lambda g: (0, 0)), pl.BlockSpec((8, 2 * state), lambda g: (0, 0)),
        ],
        out_shape=[
            jax.ShapeDtypeStruct(p.shape, BF16), jax.ShapeDtypeStruct((count, group, span, width), BF16),
            jax.ShapeDtypeStruct((16, width), F32), jax.ShapeDtypeStruct((8, 2 * state), F32),
        ],
        scratch_shapes=[
            pltpu.VMEM((count, span, width), F32), pltpu.VMEM((count, state, width), F32),
            pltpu.VMEM((state, width), F32), pltpu.VMEM((8, width), F32), pltpu.VMEM((8, 2 * state), F32),
            pltpu.VMEM((state, width), F32),
        ],
        compiler_params=pltpu.CompilerParams(vmem_limit_bytes=60 << 20),
    )(prefix, *ins, *params)


def rms(x, gain):
    return x * lax.rsqrt(jnp.mean(x * x, axis=-1, keepdims=True) + EPSILON) * gain


def body(
    tokens, norm_gain, w_gate_in, w_x_in, w_bc_in, w_dt_in, conv_x_w, conv_x_b, conv_bc_w, conv_bc_b,
    dt_bias, a_log, d_skip, gate_gain, w_out, prefix_len, cotangent,
):
    sq, hd = lax.axis_size("seq"), lax.axis_size("head")
    me_seq, me_head = lax.axis_index("seq"), lax.axis_index("head")
    micro, seqs, span, model = tokens.shape
    group = micro * seqs
    rows_here = group * span
    own_rows = rows_here // hd
    half = w_x_in.shape[1]
    width = half // sq
    heads = w_dt_in.shape[1] // sq
    state = w_bc_in.shape[1] // 2
    full_inner = half * hd
    prefix = prefix_len.reshape(group)
    everyone = ("seq", "head")

    def mine(x):
        return lax.dynamic_slice_in_dim(x.reshape(rows_here, model), me_head * own_rows, own_rows, 0)

    def blocks(x):
        return x.reshape(sq, group, span, -1)

    my_tokens = mine(tokens).astype(F32)
    my_cot = mine(cotangent)
    normed = lax.all_gather(rms(my_tokens, norm_gain).astype(BF16), everyone, axis=0, tiled=True)

    def columns(w):
        return lax.all_gather(
            lax.all_to_all(w, "seq", split_axis=1, concat_axis=0, tiled=True), "dp", axis=0, tiled=True
        )

    wd = lax.dynamic_slice_in_dim(
        lax.all_gather(w_dt_in, ("dp", "seq"), axis=0, tiled=True), me_seq * heads, heads, 1
    )
    wb = lax.all_gather(w_bc_in, ("dp", "seq"), axis=0, tiled=True)
    wcat = jnp.concatenate(
        [columns(w_gate_in), columns(w_x_in), wb, jnp.pad(wd, ((0, 0), (0, 128 - heads)))], axis=1
    )
    wo = lax.all_gather(
        lax.all_to_all(w_out, "seq", split_axis=0, concat_axis=1, tiled=True), "dp", axis=1, tiled=True
    )
    cot = lax.all_gather(my_cot, everyone, axis=0, tiled=True)

    def part(x, size, axis):
        return lax.dynamic_slice_in_dim(x, me_seq * size, size, axis)

    def spread(x):
        return jnp.repeat(part(x, heads, 0), width // heads)[None]

    params = (
        part(conv_x_w, width, 1), part(conv_x_b, width, 0)[None], conv_bc_w, conv_bc_b[None],
        spread(dt_bias), spread(-jnp.exp(a_log)), spread(d_skip), part(gate_gain, width, 0)[None],
    )
    p = blocks(jnp.dot(normed, wcat, preferred_element_type=F32).astype(BF16))
    gs = blocks(jnp.einsum("rd,kd->rk", cot, wo, preferred_element_type=F32))
    *saved, sums = ssd_forward(heads, state, prefix, p, gs, params)
    totals = lax.psum(sums, everyone)
    g, scaled, small, smallbc = ssd_backward(heads, state, full_inner, prefix, p, gs, saved, totals, params)
    g = g.reshape(sq * rows_here, -1)
    scaled = scaled.reshape(sq * rows_here, width)
    branch = lax.psum_scatter(
        jnp.dot(scaled, wo, preferred_element_type=F32).astype(BF16), everyone, scatter_dimension=0, tiled=True
    )
    result_own = (my_tokens + branch.astype(F32)).astype(BF16)
    part_normed = jnp.einsum("rc,kc->rk", g, wcat, preferred_element_type=F32)
    grad_normed = lax.psum_scatter(
        part_normed.astype(BF16), everyone, scatter_dimension=0, tiled=True
    ).astype(F32)
    gw = jnp.einsum("rk,rc->kc", normed, g, preferred_element_type=F32)
    g_wo = jnp.einsum("rk,rd->kd", scaled, cot, preferred_element_type=F32)
    grad_norm = jnp.sum(gw * wcat.astype(F32), axis=1) / norm_gain
    _, pull_norm = jax.vjp(lambda x: rms(x, norm_gain), my_tokens)
    grad_own = my_cot.astype(F32) + pull_norm(grad_normed)[0]

    def home(x):
        return lax.all_to_all(
            lax.psum_scatter(x, "dp", scatter_dimension=0, tiled=True),
            "seq", split_axis=0, concat_axis=1, tiled=True,
        )

    g_gate, g_x = (home(gw[:, at : at + width].astype(BF16)).astype(F32) for at in (0, width))
    g_dt = home(gw[:, 2 * width + 2 * state :][:, :heads])
    g_bc = lax.psum_scatter(
        lax.psum(gw[:, 2 * width : 2 * width + 2 * state], "head"), ("dp", "seq"), scatter_dimension=0, tiled=True
    )
    g_out = lax.all_to_all(
        lax.psum_scatter(g_wo.astype(BF16), "dp", scatter_dimension=1, tiled=True),
        "seq", split_axis=1, concat_axis=0, tiled=True,
    ).astype(F32)

    def whole(x):
        return lax.all_gather(x, "head", axis=0, tiled=True).reshape(micro, seqs, span, model)

    def per_head(x):
        return x.reshape(heads, width // heads)

    small = lax.all_gather(lax.psum(small, "dp"), "seq", axis=1, tiled=True)
    s_norm, s_bc = lax.psum((grad_norm, smallbc), ("dp", "seq", "head"))
    by_head = small.reshape(16, sq * heads, width // heads)
    return (
        whole(result_own), whole(grad_own), s_norm, g_gate, g_x, g_bc, g_dt,
        small[:4], small[4], s_bc[:4], s_bc[4], by_head[6, :, 0], by_head[7, :, 0], by_head[8].sum(-1), small[5], g_out,
    )


def solution(mesh):
    rows = P(("dp", "seq"), "head")
    tok = P(None, "dp", "seq", None)
    return jax.shard_map(
        body,
        mesh=mesh,
        in_specs=(
            tok, P(), rows, rows, P(("dp", "seq"), None), rows, P(None, "head"), P("head"), P(), P(),
            P("head"), P("head"), P("head"), P("head"), P("head", ("dp", "seq")), P(None, "dp"), tok,
        ),
        out_specs=(
            tok, tok, P(), rows, rows, P(("dp", "seq"), None), rows, P(None, "head"), P("head"), P(), P(),
            P("head"), P("head"), P("head"), P("head"), P("head", ("dp", "seq")),
        ),
        check_vma=False,
    )
```

time: 1110 us -> 986 us (0.89)
  waiting for transfers between devices: 390 us -> 625 us
  blocking collectives: 277 us -> 131 us
  other arithmetic: 145 us -> 7.12 us
  matrix products: 176 us -> 59.3 us
  Pallas kernels: 0 us -> 60.3 us
  local copies, waits for them, and re-layouts: 72 us -> 48.9 us
    dot_general x32 -> x6, matrix products: 169 us -> 59.3 us  [the longest x1 13.4 us: body(): gw = jnp.einsum('rk,rc->kc', normed, g, preferred_element_type=F32)]
    another operation x5 -> x0, other arithmetic: 95.8 us -> none  [the longest x2 94.9 us: mixer(): cum = jnp.cumsum(dt * -jnp.exp(a_log), axis=2)]
    psum x1 -> x2, waiting for transfers between devices: 0.01 us -> 82.9 us  [the longest x1 82.9 us: body(): totals = lax.psum(sums, everyone)]
    all_gather x1, waiting for transfers between devices: 0.02 us -> 76.2 us  [body(): lax.all_gather(rms(my_tokens, norm_gain).astype(BF16), everyone, axis=0,...]
    pallas_call x0 -> x2, Pallas kernels: none -> 60.3 us  [the longest x1 35.5 us: ssd_backward(): pl.pallas_call(functools.partial(backward_kernel, heads, state, full_inne...]
    psum x3 -> x2, blocking collectives: 111 us -> 54.7 us  [the longest x1 49 us: body(): s_norm, s_bc = lax.psum((grad_norm, smallbc), ('dp', 'seq', 'head'))]
    all_gather x1, waiting for transfers between devices: 76.2 us -> 20.2 us  [body(): cot = lax.all_gather(my_cot, everyone, axis=0, tiled=True)]
    all_gather x1, waiting for transfers between devices: 4.14 us -> 45.6 us  [body(): wb = lax.all_gather(w_bc_in, ('dp', 'seq'), axis=0, tiled=True)]
  transfers between devices with their start and end apart: 21 -> 23, of which waited for: 10 -> 15; matrix products, arithmetic and copies ran while one was open for 16% -> 8% of each run, Pallas kernels for 0% -> 0%
where the time goes in v2:
time: 986 us; the launch traced here: 983 us
  waiting for transfers between devices  625 us (63%)
  blocking collectives  131 us (13%)
  Pallas kernels  60.3 us (6%)
  matrix products  59.3 us (6%)
  local copies, waits for them, and re-layouts  48.9 us (5%)
  starting transfers between devices  36.9 us (4%)
  between operations  14.2 us (1%)
    reduce_scatter x1, waiting for transfers between devices, body(): lax.psum_scatter(part_normed.astype(BF16), everyone, scatter_dimension=0,...  123 us
    reduce_scatter x1, waiting for transfers between devices, body(): lax.psum_scatter(jnp.dot(scaled, wo, preferred_element_type=F32).astype(B...  108 us
    psum x1, waiting for transfers between devices, body(): totals = lax.psum(sums, everyone)  82.9 us
    all_gather x1, waiting for transfers between devices, body(): lax.all_gather(rms(my_tokens, norm_gain).astype(BF16), everyone, axis=0,...  76.2 us
    psum x1, blocking collectives, body(): s_norm, s_bc = lax.psum((grad_norm, smallbc), ('dp', 'seq', 'head'))  49 us
    all_gather x2, waiting for transfers between devices, columns(): lax.all_gather(lax.all_to_all(w, 'seq', split_axis=1, concat_axis=0, tile...  47 us
    all_gather x1, waiting for transfers between devices, body(): wb = lax.all_gather(w_bc_in, ('dp', 'seq'), axis=0, tiled=True)  45.6 us
    all_gather x1, blocking collectives, body(): lax.all_gather(w_dt_in, ('dp', 'seq'), axis=0, tiled=True)  36.5 us
  transfers between devices with their start and end apart: 23, of which 15 were waited for; matrix products, arithmetic and copies ran while one was open for 8% of the time, Pallas kernels for 0%

profile of v2, /device:TPU:19, one launch (start us, length us, event | category | flops | bytes accessed | tf_op | source)
XLA Modules:
  0.0 982.9 jit_solution(11702240621349398240)
XLA Ops:
  7.3 16.8 %all_to_all.115 = bf16[8,256,128]{2,1,0:T(8,128)(2,1)S(1)} all-to-all(bf16[8,256,128]{2,1,0:T(8,128)(2,1)} %bitcast.96), channel_id=1, replica_groups=mesh['dp'=2,'seq'=8,'head'=2] {'seq'}, dimensions={0} | all-to-all | bytes 1048576 | tf_op jit(solution)/shard_map/all_to_all | solution.py:387
  24.1 1.0 copy.75
  25.2 1.9 constant_dynamic-slice_fusion.1
  27.1 1.6 copy.74
  28.7 2.0 copy.70
  30.8 6.7 all-to-all-start
  37.5 2.0 copy.72
  39.5 8.7 all-to-all-done
  48.2 7.3 all-to-all-start.1
  55.6 0.9 copy_bitcast_fusion.1
  56.5 12.5 %all-to-all-done.1 = bf16[128,8,256]{0,2,1:T(8,128)(2,1)S(1)} async-done(((bf16[128,8,256]{0,2,1:T(8,128)(2,1)}), bf16[128,8,256]{0,2,1:T(8,128)(2,1)S(1)}, u32[]{:S(2)}, u32[]{:S(2)}) %all-to-all-start.1) | async-done | bytes 524320 | tf_op jit(solution)/shard_map/all_to_all | solution.py:376
  69.0 0.9 copy_bitcast_fusion
  70.2 1.0 fusion.5
  71.5 1.3 dynamic_slice.31
  72.8 1.3 dynamic_slice.35
  74.2 0.6 broadcast_in_dim_reshape.11.dsk
  76.3 36.5 %all_gather.34 = bf16[2048,32]{0,1:T(8,128)(2,1)S(1)} all-gather(bf16[128,32]{0,1:T(8,128)(2,1)S(1)} %copy-done.9), channel_id=1, replica_groups=mesh['dp'=2,'seq'=8,'head'=2] {'dp','seq'}, dimensions={0}, use_global_device_ids=true | all-gather | bytes 139264 | tf_op jit(solution)/shard_map/all_gather | solution.py:380
  113.4 20.2 %all-gather.17.cloned.1.call-done = bf16[2048,2048]{1,0:T(8,128)(2,1)} async-done(((bf16[128,2048]{1,0:T(8,128)(2,1)}), bf16[2048,2048]{1,0:T(8,128)(2,1)}) %all-gather.17.cloned.1.call-update) | async-done | bytes 8388624 | tf_op jit(solution)/shard_map/all_gather | solution.py:389
  133.6 7.3 fusion.15
  140.9 45.6 %all-gather.15.cloned.1.call-done = bf16[2048,256]{0,1:T(8,128)(2,1)} async-done(((bf16[128,256]{0,1:T(8,128)(2,1)}), bf16[2048,256]{0,1:T(8,128)(2,1)}) %all-gather.15.cloned.1.call-update) | async-done | bytes 1048592 | tf_op jit(solution)/shard_map/all_gather | solution.py:382
  186.5 23.7 %all-gather.11.cloned.1.call-done = bf16[2048,256]{0,1:T(8,128)(2,1)} async-done(((bf16[1024,256]{0,1:T(8,128)(2,1)}), bf16[2048,256]{0,1:T(8,128)(2,1)}) %all-gather.11.cloned.1.call-update) | async-done | bytes 1048592 | tf_op jit(solution)/shard_map/all_gather | solution.py:375
  210.2 23.3 %all-gather.13.cloned.1.call-done = bf16[2048,256]{0,1:T(8,128)(2,1)} async-done(((bf16[1024,256]{0,1:T(8,128)(2,1)}), bf16[2048,256]{0,1:T(8,128)(2,1)}) %all-gather.13.cloned.1.call-update) | async-done | bytes 1048592 | tf_op jit(solution)/shard_map/all_gather | solution.py:375
  233.5 76.2 %all-gather.9.cloned.1.call-done = bf16[2048,2048]{1,0:T(8,128)(2,1)} async-done(((bf16[128,2048]{1,0:T(8,128)(2,1)}), bf16[2048,2048]{1,0:T(8,128)(2,1)}) %all-gather.9.cloned.1.call-update) | async-done | bytes 8388624 | tf_op jit(solution)/shard_map/all_gather | solution.py:372
  309.7 13.4 %convolution_convert_fusion.2 = bf16[2048,896]{1,0:T(8,128)(2,1)} fusion(bf16[2048,2048]{1,0:T(8,128)(2,1)} %all-gather.9.cloned.1.call-done, bf16[2048,4]{0,1:T(4,128)(2,1)S(1)} %constant_dynamic-slice_fusion.2, bf16[2048,256]{0,1:T(8,128)(2,1)} %all-gather.15.cloned.1.call-done, bf16[2048,256]{0,1:T(8,128)(2,1)} %all-gather.13.cloned.1.call-done, ...), kind=kOutput, calls=%fused_computation.6 | convolution fusion | flops 7536377856 | bytes 15220736 | tf_op jit(solution)/shard_map/dot_general | solution.py:401
  323.1 24.9 %shard_map.288 = (f32[8,2,128,256]{3,2,1,0:T(8,128)}, f32[8,2,128,256]{3,2,1,0:T(8,128)}, f32[8,2,128,256]{3,2,1,0:T(8,128)}, f32[8,2,128,256]{3,2,1,0:T(8,128)}...) custom-call(s32[2]{0:T(128)} %bitcast.106, ...), custom_call_target="tpu_custom_call" | custom-call | tf_op jit(solution)/shard_map/pallas_call | solution.py:303
  348.2 82.9 %all-reduce.5.cloned.1.call-done.tot_ref = f32[8,2,8,128]{3,2,1,0:T(8,128)} async-done(((f32[8,2,8,128]{3,2,1,0:T(8,128)}), f32[8,2,8,128]{3,2,1,0:T(8,128)}) %all-reduce.5.cloned.1.call-update) | async-done | bytes 65552 | tf_op jit(solution)/shard_map/psum | solution.py:404
  431.1 35.5 %shard_map.289 = (bf16[8,2,128,896]{3,2,1,0:T(8,128)(2,1)}, bf16[8,2,128,256]{3,2,1,0:T(8,128)(2,1)}, f32[16,256]{1,0:T(8,128)}, f32[8,256]{1,0:T(8,128)}) custom-call(s32[2]{0:T(128)} %bitcast.107, bf16[8,2,128,896]{3,2,1,0:T(8,128)(2,1)} %bitcast.78, f32[8,2,128,256]{3,2,1,0:T(8,128)} %bitcast.82, f32[8,2,128,256]{3,2,1,0:T(8,128)} %get-tuple-element.28.xc_ref, ...), custom_call_target="tpu_custom_call" | custom-call | tf_op jit(solution)/shard_map/pallas_call | solution.py:319
  466.6 13.4 %fusion.11 = (bf16[2048,896]{0,1:T(8,128)(2,1)}, f32[2048]{0:T(1024)S(1)}, f32[2048,896]{0,1:T(8,128)S(1)}) fusion(bf16[2048,4]{0,1:T(4,128)(2,1)S(1)} %constant_dynamic-slice_fusion.2, bf16[2048,256]{0,1:T(8,128)(2,1)S(1)} %copy-done.11, bf16[2048,256]{0,1:T(8,128)(2,1)} %all-gather.13.cloned.1.call-done, bf16[2048,256]{0,1:T(8,128)(2,1)S(1)} %copy-done.12, ...), kind=kOutput, calls=%fused_computation.34 | convolution fusion | flops 7540045824 | bytes 26238976 | tf_op jit(solution)/shard_map/rk,rc->kc/dot_general | solution.py:416
  480.0 2.9 copy-done.6
  483.0 1.5 slice.55
  484.5 12.7 %convolution_convert_fusion = bf16[2048,2048]{1,0:T(8,128)(2,1)} fusion(bf16[2048,896]{1,0:T(8,128)(2,1)} %bitcast.112, bf16[2048,4]{0,1:T(4,128)(2,1)S(1)} %constant_dynamic-slice_fusion.2, bf16[2048,256]{0,1:T(8,128)(2,1)S(1)} %copy-done.11, bf16[2048,256]{0,1:T(8,128)(2,1)} %all-gather.13.cloned.1.call-done, bf16[2048,256]{0,1:T(8,128)(2,1)S(1)} %copy-done.12), kind=kOutput, calls=%fused_computation | convolution fusion | flops 7538737152 | bytes 15220736 | tf_op jit(solution)/shard_map/rc,kc->rk/dot_general | solution.py:412
  497.3 1.2 copy-done.2
  498.8 5.7 convolution_convert_fusion.1
  504.5 0.8 slice.56
  505.4 1.3 copy.87
  506.8 3.1 fusion.12
  510.0 0.7 reduce-scatter.16.cloned.1.call-update
  511.0 6.8 convolution_convert_fusion.3
  517.8 33.4 %reduce-scatter.20.cloned.1.call-done = f32[128,256]{0,1:T(8,128)} async-done(((f32[2048,256]{0,1:T(8,128)}), f32[128,256]{0,1:T(8,128)}) %reduce-scatter.20.cloned.1.call-update) | async-done | bytes 131088 | tf_op jit(solution)/shard_map/reduce_scatter | solution.py:430
  551.3 122.9 %reduce-scatter.12.cloned.1.call-done = bf16[128,2048]{1,0:T(8,128)(2,1)} async-done(((bf16[2048,2048]{1,0:T(8,128)(2,1)}), bf16[128,2048]{1,0:T(8,128)(2,1)}) %reduce-scatter.12.cloned.1.call-update) | async-done | bytes 524304 | tf_op jit(solution)/shard_map/reduce_scatter | solution.py:413
  674.2 1.3 fusion.7
  675.5 107.6 %reduce-scatter.10.cloned.1.call-done = bf16[128,2048]{1,0:T(8,128)(2,1)} async-done(((bf16[2048,2048]{1,0:T(8,128)(2,1)}), bf16[128,2048]{1,0:T(8,128)(2,1)}) %reduce-scatter.10.cloned.1.call-update) | async-done | bytes 524304 | tf_op jit(solution)/shard_map/reduce_scatter | solution.py:408
  783.1 2.8 fusion.2
  786.0 20.3 %reduce-scatter.22.cloned.1.call-done = f32[1024,4]{1,0:T(8,128)} async-done(((f32[2048,4]{1,0:T(8,128)}), f32[1024,4]{1,0:T(8,128)}) %reduce-scatter.22.cloned.1.call-update) | async-done | bytes 16400
  806.3 1.8 copy.88
  808.1 5.5 all-to-all-start.5
  813.6 15.7 %reduce-scatter.14.cloned.1.call-done = bf16[1024,256]{0,1:T(8,128)(2,1)} async-done(((bf16[2048,256]{0,1:T(8,128)(2,1)}), bf16[1024,256]{0,1:T(8,128)(2,1)}) %reduce-scatter.14.cloned.1.call-update) | async-done | bytes 524304 | tf_op jit(solution)/shard_map/reduce_scatter | solution.py:424
  829.3 1.9 copy_bitcast_fusion.4
  831.3 5.5 all-to-all-start.3
  837.3 15.3 %reduce-scatter.16.cloned.1.call-done = bf16[1024,256]{0,1:T(8,128)(2,1)} async-done(((bf16[2048,256]{0,1:T(8,128)(2,1)}), bf16[1024,256]{0,1:T(8,128)(2,1)}) %reduce-scatter.16.cloned.1.call-update) | async-done | bytes 524304 | tf_op jit(solution)/shard_map/reduce_scatter | solution.py:424
  852.6 1.9 copy_bitcast_fusion.3
  854.6 5.5 all-to-all-start.4
  860.0 15.1 %reduce-scatter.18.cloned.1.call-done = bf16[256,1024]{1,0:T(8,128)(2,1)} async-done(((bf16[256,2048]{1,0:T(8,128)(2,1)}), bf16[256,1024]{1,0:T(8,128)(2,1)}) %reduce-scatter.18.cloned.1.call-update) | async-done | bytes 524304 | tf_op jit(solution)/shard_map/reduce_scatter | solution.py:434
  875.1 1.9 copy_bitcast_fusion.2
  877.0 5.5 all-to-all-start.6
  882.5 5.8 psum.38
  888.3 23.2 %all_gather.39 = f32[16,2048]{1,0:T(8,128)S(1)} all-gather(f32[16,256]{1,0:T(8,128)S(1)} %psum.38), channel_id=1, replica_groups=mesh['dp'=2,'seq'=8,'head'=2] {'seq'}, dimensions={1}, use_global_device_ids=true | all-gather | bytes 147456 | tf_op jit(solution)/shard_map/all_gather | solution.py:444
  912.2 49.0 %all-reduce.1 = (f32[2048]{0:T(1024)}, f32[8,256]{1,0:T(8,128)S(1)}) all-reduce(f32[2048]{0:T(1024)S(1)} %div.19, f32[8,256]{1,0:T(8,128)S(1)} %copy-done.10), channel_id=1, replica_groups=mesh['dp'=2,'seq'=8,'head'=2] {'dp','seq','head'}, use_global_device_ids=true, to_apply=%region_6.7 | all-reduce | flops 4096 | bytes 32768 | tf_op jit(solution)/shard_map/psum | solution.py:445
  964.9 1.3 copy.85
  966.3 1.3 copy.84
  967.6 1.0 convert_element_type.89
  968.6 1.7 copy.86
  970.3 2.3 copy.106
  972.6 3.1 copy.107
  (99 shorter events, 9.9 us)
Async XLA Ops:
  7.2 105.6 %copy-start = (f32[4,2048]{1,0:T(4,128)S(1)}, f32[4,2048]{1,0:T(4,128)}, u32[]{:S(2)}) copy-start(f32[4,2048]{1,0:T(4,128)} %param.23) | copy-start | bytes 98308
  7.2 62.7 %copy-start.3 = (bf16[2,1,128,2048]{3,2,1,0:T(8,128)(2,1)S(1)}, bf16[2,1,128,2048]{3,2,1,0:T(8,128)(2,1)}, u32[]{:S(2)}) copy-start(bf16[2,1,128,2048]{3,2,1,0:T(8,128)(2,1)} %param.17) | copy-start | bytes 3145732
  7.2 62.9 %copy-start.7 = (f32[2048]{0:T(1024)S(1)}, f32[2048]{0:T(1024)}, u32[]{:S(2)}) copy-start(f32[2048]{0:T(1024)} %param.18) | copy-start | bytes 24580
  7.2 64.0 %copy-start.13 = (f32[32]{0:T(128)S(1)}, f32[32]{0:T(128)}, u32[]{:S(2)}) copy-start(f32[32]{0:T(128)} %param.27) | copy-start | bytes 388
  7.2 64.1 %copy-start.14 = (f32[32]{0:T(128)S(1)}, f32[32]{0:T(128)}, u32[]{:S(2)}) copy-start(f32[32]{0:T(128)} %param.28) | copy-start | bytes 388
  7.2 64.2 %copy-start.15 = (f32[32]{0:T(128)S(1)}, f32[32]{0:T(128)}, u32[]{:S(2)}) copy-start(f32[32]{0:T(128)} %param.29) | copy-start | bytes 388
  7.2 69.0 %copy-start.9 = (bf16[128,32]{0,1:T(8,128)(2,1)S(1)}, bf16[128,32]{0,1:T(8,128)(2,1)}, u32[]{:S(2)}) copy-start(bf16[128,32]{0,1:T(8,128)(2,1)} %param.22) | copy-start | bytes 24580
  7.3 106.1 %all-gather.19.cloned.1.call-start = ((), (), s32[]{:S(2)}) async-start(), calls=%async_computation.19 | async-start | bytes 1572864 | tf_op jit(solution)/shard_map/all_gather | solution.py:386
  25.1 108.5 %all-gather.17.cloned.1.call-start = ((), (), s32[]{:S(2)}) async-start(), calls=%async_computation.18 | async-start | bytes 8912896 | tf_op jit(solution)/shard_map/all_gather | solution.py:389
  27.1 159.4 %all-gather.15.cloned.1.call-start = ((), (), s32[]{:S(2)}) async-start(), calls=%async_computation.17 | async-start | bytes 1114112 | tf_op jit(solution)/shard_map/all_gather | solution.py:382
  30.8 17.5 %all-to-all-start = ((bf16[128,8,256]{0,2,1:T(8,128)(2,1)}), bf16[128,8,256]{0,2,1:T(8,128)(2,1)S(1)}, u32[]{:S(2)}, u32[]{:S(2)}) async-start(bf16[128,8,256]{0,2,1:T(8,128)(2,1)} %bitcast.2), calls=%async_computation | async-start | bytes 1048576 | tf_op jit(solution)/shard_map/all_to_all | solution.py:376
  48.2 20.7 %all-to-all-start.1 = ((bf16[128,8,256]{0,2,1:T(8,128)(2,1)}), bf16[128,8,256]{0,2,1:T(8,128)(2,1)S(1)}, u32[]{:S(2)}, u32[]{:S(2)}) async-start(bf16[128,8,256]{0,2,1:T(8,128)(2,1)} %bitcast.4), calls=%async_computation.1 | async-start | bytes 1048576 | tf_op jit(solution)/shard_map/all_to_all | solution.py:376
  55.6 154.6 %all-gather.11.cloned.1.call-start = ((), (), s32[]{:S(2)}) async-start(), calls=%async_computation.15 | async-start | bytes 1572864 | tf_op jit(solution)/shard_map/all_gather | solution.py:375
  56.5 177.0 %all-gather.13.cloned.1.call-start = ((), (), s32[]{:S(2)}) async-start(), calls=%async_computation.16 | async-start | bytes 1572864 | tf_op jit(solution)/shard_map/all_gather | solution.py:375
  69.9 239.8 %all-gather.9.cloned.1.call-start = ((), (), s32[]{:S(2)}) async-start(), calls=%async_computation.14 | async-start | bytes 8912896 | tf_op jit(solution)/shard_map/all_gather | solution.py:372
  71.2 359.9 %all-reduce.5.cloned.1.call-start = ((), (), s32[]{:S(2)}) async-start(), calls=%async_computation.20 | async-start | bytes 131072 | tf_op jit(solution)/shard_map/psum | solution.py:404
  348.0 203.3 %reduce-scatter.20.cloned.1.call-start = ((), (), s32[]{:S(2)}) async-start(), calls=%async_computation.28 | async-start | bytes 2228224 | tf_op jit(solution)/shard_map/reduce_scatter | solution.py:430
  431.1 35.5 %copy-start.11 = (bf16[2048,256]{0,1:T(8,128)(2,1)S(1)}, bf16[2048,256]{0,1:T(8,128)(2,1)}, u32[]{:S(2)}) copy-start(bf16[2048,256]{0,1:T(8,128)(2,1)} %all-gather.15.cloned.1.call-done) | copy-start | bytes 3145732
  431.1 35.5 %copy-start.12 = (bf16[2048,256]{0,1:T(8,128)(2,1)S(1)}, bf16[2048,256]{0,1:T(8,128)(2,1)}, u32[]{:S(2)}) copy-start(bf16[2048,256]{0,1:T(8,128)(2,1)} %all-gather.11.cloned.1.call-done) | copy-start | bytes 3145732
  480.0 2.9 copy-start.6
  484.5 189.8 %reduce-scatter.12.cloned.1.call-start = ((), (), s32[]{:S(2)}) async-start(), calls=%async_computation.23 | async-start | bytes 8912896 | tf_op jit(solution)/shard_map/reduce_scatter | solution.py:413
  497.2 1.2 copy-start.2
  497.2 1.5 copy-start.5
  497.3 285.9 %reduce-scatter.10.cloned.1.call-start = ((), (), s32[]{:S(2)}) async-start(), calls=%async_computation.21 | async-start | bytes 8912896 | tf_op jit(solution)/shard_map/reduce_scatter | solution.py:408
  504.5 301.8 %reduce-scatter.22.cloned.1.call-start = ((), (), s32[]{:S(2)}) async-start(), calls=%async_computation.30 | async-start | bytes 1572864
  506.7 322.6 %reduce-scatter.14.cloned.1.call-start = ((), (), s32[]{:S(2)}) async-start(), calls=%async_computation.25 | async-start | bytes 1572864 | tf_op jit(solution)/shard_map/reduce_scatter | solution.py:424
  509.9 342.7 %reduce-scatter.16.cloned.1.call-start = ((), (), s32[]{:S(2)}) async-start(), calls=%async_computation.26 | async-start | bytes 1572864 | tf_op jit(solution)/shard_map/reduce_scatter | solution.py:424
  510.7 272.5 %copy-start.4 = (bf16[2,1,128,2048]{3,2,1,0:T(8,128)(2,1)S(1)}, bf16[2,1,128,2048]{3,2,1,0:T(8,128)(2,1)}, u32[]{:S(2)}) copy-start(bf16[2,1,128,2048]{3,2,1,0:T(8,128)(2,1)} %param.33) | copy-start | bytes 3145732
  510.7 364.4 %reduce-scatter.18.cloned.1.call-start = ((), (), s32[]{:S(2)}) async-start(), calls=%async_computation.27 | async-start | bytes 1572864 | tf_op jit(solution)/shard_map/reduce_scatter | solution.py:434
  517.8 364.7 %copy-start.8 = (f32[16,256]{1,0:T(8,128)S(1)}, f32[16,256]{1,0:T(8,128)}, u32[]{:S(2)}) copy-start(f32[16,256]{1,0:T(8,128)} %get-tuple-element.38) | copy-start | bytes 49156
  517.8 394.4 %copy-start.10 = (f32[8,256]{1,0:T(8,128)S(1)}, f32[8,256]{1,0:T(8,128)}, u32[]{:S(2)}) copy-start(f32[8,256]{1,0:T(8,128)} %get-tuple-element.39) | copy-start | bytes 24580
  517.8 450.8 %all-reduce.7.cloned.1.call-start = ((), (), s32[]{:S(2)}) async-start(), calls=%async_computation.29 | async-start | bytes 262144 | tf_op jit(solution)/shard_map/psum | solution.py:431
  551.3 419.0 %all-gather.21.cloned.1.call-start = ((), (), s32[]{:S(2)}) async-start(), calls=%async_computation.22 | async-start | bytes 1572864 | tf_op jit(solution)/shard_map/all_gather | solution.py:439
  808.1 23.1 %all-to-all-start.5 = ((f32[8,128,4]{1,2,0:T(4,128)}), f32[8,128,4]{1,2,0:T(4,128)S(1)}, u32[]{:S(2)}, u32[]{:S(2)}) async-start(f32[8,128,4]{1,2,0:T(4,128)} %bitcast.25), calls=%async_computation.9 | async-start | bytes 32768 | tf_op jit(solution)/shard_map/all_to_all | solution.py:423
  831.3 23.3 %all-to-all-start.3 = ((bf16[8,128,256]{1,2,0:T(8,128)(2,1)}), bf16[8,128,256]{1,2,0:T(8,128)(2,1)S(1)}, u32[]{:S(2)}, u32[]{:S(2)}) async-start(bf16[8,128,256]{1,2,0:T(8,128)(2,1)} %copy_bitcast_fusion.4), calls=%async_computation.6 | async-start | bytes 1048576 | tf_op jit(solution)/shard_map/all_to_all | solution.py:423
  836.7 133.6 %all-gather.23.cloned.1.call-start = ((), (), s32[]{:S(2)}) async-start(), calls=%async_computation.24 | async-start | bytes 3145728 | tf_op jit(solution)/shard_map/all_gather | solution.py:439
  854.6 22.5 %all-to-all-start.4 = ((bf16[8,128,256]{1,2,0:T(8,128)(2,1)}), bf16[8,128,256]{1,2,0:T(8,128)(2,1)S(1)}, u32[]{:S(2)}, u32[]{:S(2)}) async-start(bf16[8,128,256]{1,2,0:T(8,128)(2,1)} %copy_bitcast_fusion.3), calls=%async_computation.8 | async-start | bytes 1048576 | tf_op jit(solution)/shard_map/all_to_all | solution.py:423
  877.0 90.6 %all-to-all-start.6 = ((bf16[256,8,128]{2,0,1:T(8,128)(2,1)}), bf16[256,8,128]{2,0,1:T(8,128)(2,1)S(1)}, u32[]{:S(2)}, u32[]{:S(2)}) async-start(bf16[256,8,128]{2,0,1:T(8,128)(2,1)} %copy_bitcast_fusion.2), calls=%async_computation.11 | async-start | bytes 1048576 | tf_op jit(solution)/shard_map/all_to_all | solution.py:433
  964.8 11.5 %copy-start.1 = (f32[4,2048]{1,0:T(4,128)S(1)}, f32[4,2048]{1,0:T(4,128)}, u32[]{:S(2)}) copy-start(f32[4,2048]{1,0:T(4,128)} %param.23) | copy-start | bytes 98308
Sparse Core Ops, SparseCore 0:
  25.3 23.8 all-gather.18
  51.8 81.7 all-gather.16
  136.9 49.5 all-gather.14
  188.5 21.6 all-gather.10
  212.1 21.2 all-gather.12
  236.1 73.5 all-gather.8
  348.1 82.9 all-reduce.4
  484.6 66.6 reduce-scatter.19
  555.9 118.3 reduce-scatter.11
  678.7 104.4 reduce-scatter.9
  786.1 20.2 reduce-scatter.21
  809.0 20.3 reduce-scatter.13
  832.2 20.3 reduce-scatter.15
  854.7 20.3 reduce-scatter.17
  877.3 18.6 all-reduce.6
  898.0 10.1 all-gather.20
  910.3 11.7 all-gather.22

commit v3 on v2

--- a/solution.py
+++ b/solution.py
@@ -54,6 +54,10 @@
 
 def one_hot(cond):
     return jnp.where(cond, 1.0, 0.0).astype(BF16)
+
+
+def column(row):
+    return jnp.broadcast_to(row, (8, row.shape[1])).T[:, 0:1]
 
 
 def conv_window(p_ref, k, lo, hi):
@@ -144,7 +148,8 @@
         ones = jnp.ones((8, width), BF16)
         square = mm_left(ones, gated * gated, 2, NT)
         cross = mm_left(ones, gated * (gs_ref[k, 0] * gain[...]), 2, NT)
-        sums_ref[k, 0] = jnp.where(iota((8, span), 0) == 0, square, cross)
+        sums_ref[0, 0, pl.ds(k, 1), :] = square[0:1]
+        sums_ref[0, 1, pl.ds(k, 1), :] = cross[0:1]
         return carry
 
     lax.fori_loop(0, count, descend, 0)
@@ -176,9 +181,8 @@
         ref[...] = jnp.zeros_like(ref)
 
     def ascend(k, carry):
-        tot = tot_ref[k, 0].T
-        mean_sq = tot[:, 0:1] * (1.0 / full_inner)
-        mean_x = tot[:, 1:2] * (1.0 / full_inner)
+        mean_sq = column(tot_ref[0, 0, pl.ds(k, 1), :]) * (1.0 / full_inner)
+        mean_x = column(tot_ref[0, 1, pl.ds(k, 1), :]) * (1.0 / full_inner)
         scale = lax.rsqrt(mean_sq + EPSILON)
         gate = p_ref[k, 0, :, :width].astype(F32)
         sig = sigmoid(gate)
@@ -288,6 +292,10 @@
     return pl.BlockSpec((shape[0], 1) + tuple(shape[2:]), lambda g: (0, g, 0, 0))
 
 
+def sums_block(count, span):
+    return pl.BlockSpec((1, 2, count, span), lambda g: (g, 0, 0, 0))
+
+
 def whole_block(a):
     return pl.BlockSpec(a.shape, lambda g: (0,) * a.ndim)
 
@@ -298,15 +306,15 @@
     outs = [
         (count, group, span, width), (count, group, span, 2 * state), (count, group, span, width),
         (count, group, span, width), (count, group, span, width), (count, group, state, width),
-        (count, group, state, width), (count, group, 8, span),
+        (count, group, state, width),
     ]
     return pl.pallas_call(
         functools.partial(forward_kernel, heads, state),
         grid=(group,),
         in_specs=[pl.BlockSpec(memory_space=pltpu.SMEM), group_block(p.shape), group_block(gs.shape)]
         + [whole_block(a) for a in params],
-        out_specs=[group_block(o) for o in outs],
-        out_shape=[jax.ShapeDtypeStruct(o, F32) for o in outs],
+        out_specs=[group_block(o) for o in outs] + [sums_block(count, span)],
+        out_shape=[jax.ShapeDtypeStruct(o, F32) for o in outs + [(group, 2, count, span)]],
         scratch_shapes=[pltpu.VMEM((state, width), F32)] * 2,
         compiler_params=pltpu.CompilerParams(vmem_limit_bytes=56 << 20),
     )(prefix, p, gs, *params)
@@ -320,7 +328,7 @@
         functools.partial(backward_kernel, heads, state, full_inner),
         grid=(group,),
         in_specs=[pl.BlockSpec(memory_space=pltpu.SMEM)]
-        + [group_block(a.shape) for a in ins]
+        + [group_block(a.shape) for a in ins[:-1]] + [sums_block(count, span)]
         + [whole_block(a) for a in params],
         out_specs=[
             group_block(p.shape), group_block((count, group, span, width)),
@@ -339,6 +347,641 @@
     )(prefix, *ins, *params)
 
 
+def ring_place(s, n):
+    return (1 - s % 2) * (s // 2) + (s % 2) * (n - 1 - s // 2)
+
+
+def ring_index(p, n):
+    p = (p + 2 * n) % n
+    far = p // (n // 2)
+    return (1 - far) * 2 * p + far * (2 * (n - 1 - p) + 1)
+
+
+def axes_here():
+    return {a: (lax.axis_index(a), lax.axis_size(a)) for a in ("dp", "seq", "head")}
+
+
+def greet(axis_names, diagonal=False):
+    here = axes_here()
+    barrier = pltpu.get_barrier_semaphore()
+    total = 0
+    for axis in axis_names:
+        me, size = here[axis]
+        total += size - 1
+
+        def hello(k, carry, axis=axis, me=me, size=size):
+            pl.semaphore_signal(
+                barrier, inc=1, device_id={axis: (me + 1 + k) % size}, device_id_type=pl.DeviceIdType.MESH
+            )
+            return carry
+
+        lax.fori_loop(0, size - 1, hello, 0)
+    if diagonal:
+        (me_dp, dp), (me, sq) = here["dp"], here["seq"]
+        total += (dp - 1) * (sq - 1)
+
+        def across(k, carry):
+            for d in range(1, dp):
+                pl.semaphore_signal(
+                    barrier, inc=1, device_id={"dp": (me_dp + d) % dp, "seq": (me + 1 + k) % sq},
+                    device_id_type=pl.DeviceIdType.MESH,
+                )
+            return carry
+
+        lax.fori_loop(0, sq - 1, across, 0)
+    pl.semaphore_wait(barrier, total)
+
+
+def remote(src, dst, send, recv, axis, index):
+    return pltpu.make_async_remote_copy(
+        src_ref=src, dst_ref=dst, send_sem=send, recv_sem=recv,
+        device_id=dict(zip(axis, index)) if isinstance(axis, tuple) else {axis: index}, device_id_type=pl.DeviceIdType.MESH,
+    )
+
+
+def gather_kernel(
+    own_a, own_b, w3, wb, wd, all_a, all_b, w3_all, wb_all, wd_all,
+    local, r_send, r_recv, l_send, l_recv, s_send, s_recv, q_send, q_recv, d_send, d_recv,
+):
+    here = axes_here()
+    (me_dp, dp), (me, sq), (me_head, hd) = here["dp"], here["seq"], here["head"]
+    place = ring_place(me, sq)
+    right, left = ring_index(place + 1, sq), ring_index(place - 1, sq)
+    other = hd - 1 - me_head
+    half = sq // 2
+    rows = own_a.shape[0]
+    piece = rows // 2
+    width = w3_all.shape[-1]
+    greet(("dp", "seq", "head"))
+
+    pairs = ((own_a, all_a), (own_b, all_b))
+    own_copies = []
+    for i, (own, out) in enumerate(pairs):
+        own_copies.append(pltpu.make_async_copy(own, out.at[me, me_head], local.at[i]))
+    mats = (
+        (lambda s: w3.at[:, :, pl.ds(pl.multiple_of(s * width, width), width)], lambda d, s: w3_all.at[:, d, s]),
+        (lambda s: wb, lambda d, s: wb_all.at[d, s]),
+        (lambda s: wd.at[s], lambda d, s: wd_all.at[d, s]),
+    )
+    for i, (src, dst) in enumerate(mats):
+        own_copies.append(pltpu.make_async_copy(src(me), dst(me_dp, me), local.at[2 + i]))
+    for copy in own_copies:
+        copy.start()
+
+    def sub(ref, h):
+        return ref.at[pl.ds(h * piece, piece)]
+
+    def block(out, index, h):
+        return sub(out.at[index, me_head], h)
+
+    def to_sibling(i, slot, h, src, dst):
+        remote(src, dst, s_send.at[i, slot, h], s_recv.at[i, slot, h], "head", other).start()
+
+    for i, (own, out) in enumerate(pairs):
+        for h in range(2):
+            src, dst = sub(own, h), block(out, me, h)
+            remote(src, dst, r_send.at[i, 0, h], r_recv.at[i, 0, h], "seq", right).start()
+            remote(src, dst, l_send.at[i, 0, 1 - h], l_recv.at[i, 0, 1 - h], "seq", left).start()
+        if i == 0:
+            def scatter(k, carry):
+                peer = (me + 1 + k) % sq
+                for m, (src, dst) in enumerate(mats):
+                    remote(src(peer), dst(me_dp, me), q_send.at[m, k], q_recv.at[m, k], "seq", peer).start()
+                return carry
+
+            lax.fori_loop(0, sq - 1, scatter, 0)
+
+    for i, (own, out) in enumerate(pairs):
+        for h in range(2):
+            to_sibling(i, 0, h, sub(own, h), block(out, me, h))
+
+    def forward(k, carry):
+        source = (me + 2 * sq - 1 - k) % sq
+        for d in range(1, dp):
+            for m, (src, dst) in enumerate(mats):
+                remote(
+                    dst(me_dp, source), dst(me_dp, source), d_send.at[m, d - 1, k + 1], d_recv.at[m, d - 1, k + 1],
+                    "dp", (me_dp + d) % dp,
+                ).start()
+        return carry
+
+    for copy in own_copies[len(pairs):]:
+        copy.wait()
+    forward(-1, 0)
+
+    def arrived(k, carry):
+        source = (me + 2 * sq - 1 - k) % sq
+        for m, (src, dst) in enumerate(mats):
+            remote(
+                src((me + 1 + k) % sq), dst(me_dp, source), q_send.at[m, k], q_recv.at[m, k],
+                "seq", (me + 1 + k) % sq,
+            ).wait()
+        return forward(k, carry)
+
+    for hop in range(1, half + 1):
+        for i, (own, out) in enumerate(pairs):
+            from_left = ring_index(place - hop, sq)
+            from_right = ring_index(place + hop, sq)
+            for h in range(2):
+                if hop < half or h == 0:
+                    ref = block(out, from_left, h)
+                    remote(ref, ref, r_send.at[i, hop - 1, h], r_recv.at[i, hop - 1, h], "seq", right).wait_recv()
+                    if hop < half - 1 or (hop == half - 1 and h == 0):
+                        remote(ref, ref, r_send.at[i, hop, h], r_recv.at[i, hop, h], "seq", right).start()
+                    to_sibling(i, hop, h, ref, ref)
+                g = 1 - h
+                if hop < half or g == 1:
+                    ref = block(out, from_right, g)
+                    remote(ref, ref, l_send.at[i, hop - 1, h], l_recv.at[i, hop - 1, h], "seq", left).wait_recv()
+                    if hop < half - 1 or (hop == half - 1 and g == 1):
+                        remote(ref, ref, l_send.at[i, hop, h], l_recv.at[i, hop, h], "seq", left).start()
+                    if hop < half:
+                        to_sibling(i, half + hop, g, ref, ref)
+                    else:
+                        to_sibling(i, half, 1, ref, ref)
+        if hop == 1:
+            lax.fori_loop(0, sq - 1, arrived, 0)
+
+    for i, (own, out) in enumerate(pairs):
+        for hop in range(half):
+            for h in range(2):
+                if hop < half - 1 or h == 0:
+                    ref = block(out, me, h)
+                    remote(ref, ref, r_send.at[i, hop, h], r_recv.at[i, hop, h], "seq", right).wait_send()
+                    remote(ref, ref, l_send.at[i, hop, h], l_recv.at[i, hop, h], "seq", left).wait_send()
+        for slot in range(sq):
+            step = slot if slot <= half else half - slot
+            source = ring_index(place - step, sq)
+            for h in range(2):
+                mine = block(out, source, h)
+                theirs = sub(out.at[source, other], h)
+                copy = remote(mine, theirs, s_send.at[i, slot, h], s_recv.at[i, slot, h], "head", other)
+                copy.wait_send()
+                copy.wait_recv()
+
+    def last(k, carry):
+        source = (me + 2 * sq - k) % sq
+        for d in range(1, dp):
+            came = (me_dp + dp - d) % dp
+            for m, (src, dst) in enumerate(mats):
+                copy = remote(
+                    dst(me_dp, source), dst(came, source), d_send.at[m, d - 1, k], d_recv.at[m, d - 1, k],
+                    "dp", (me_dp + d) % dp,
+                )
+                copy.wait_send()
+                copy.wait_recv()
+        return carry
+
+    lax.fori_loop(0, sq, last, 0)
+    for copy in own_copies[:len(pairs)]:
+        copy.wait()
+
+
+def gather_all(own_a, own_b, w3, wb, wd, collective_id=0):
+    dp, sq, hd = lax.axis_size("dp"), lax.axis_size("seq"), lax.axis_size("head")
+    rows, model = own_a.shape
+    kinds, depth, half = w3.shape
+    width = half // sq
+    anywhere = pl.BlockSpec(memory_space=pl.ANY)
+    dma = pltpu.SemaphoreType.DMA
+    S = jax.ShapeDtypeStruct
+    return pl.pallas_call(
+        gather_kernel,
+        out_shape=[
+            S((sq, hd, rows, model), BF16), S((sq, hd, rows, model), BF16),
+            S((kinds, dp, sq, depth, width), BF16), S((dp, sq) + wb.shape, BF16), S((dp, sq) + wd.shape[1:], BF16),
+        ],
+        in_specs=[anywhere] * 5,
+        out_specs=[anywhere] * 5,
+        scratch_shapes=[
+            dma((5,)), dma((2, sq // 2, 2)), dma((2, sq // 2, 2)), dma((2, sq // 2, 2)), dma((2, sq // 2, 2)),
+            dma((2, sq, 2)), dma((2, sq, 2)), dma((3, sq)), dma((3, sq)), dma((3, dp, sq)), dma((3, dp, sq)),
+        ],
+        compiler_params=pltpu.CompilerParams(collective_id=collective_id, has_side_effects=True),
+    )(own_a, own_b, w3, wb, wd)
+
+
+def scatter_kernel(
+    parts, xs0, xs1, g3, gb, gd, small, sb,
+    out0, out1, o3, ob, od, osmall, osb,
+    own_x, sib_x, rbuf, lbuf, fin, v3, vb, vd, l3, lb, ld,
+    local, x_send, x_recv, r_send, r_recv, l_send, l_recv, f_send, f_recv,
+    d_send, d_recv, q_send, q_recv, b_send, b_recv,
+):
+    here = axes_here()
+    (me_dp, dp), (me, sq), (me_head, hd) = here["dp"], here["seq"], here["head"]
+    place = ring_place(me, sq)
+    right, left = ring_index(place + 1, sq), ring_index(place - 1, sq)
+    other = hd - 1 - me_head
+    half = sq // 2
+    rows = own_x.shape[2]
+    piece = rows // parts
+    width = v3.shape[-1]
+    near = range(parts)
+    first, second = range(parts // 2), range(parts // 2, parts)
+    xs, outs = (xs0, xs1), (out0, out1)
+    rings = range(2)
+    greet(("dp", "seq", "head"), diagonal=True)
+
+    def sub(ref, h):
+        return ref.at[pl.ds(h * piece, piece)]
+
+    order = [half]
+    for step in range(half - 1, 0, -1):
+        order += [step, -step]
+    order.append(0)
+    loads = []
+    for i in rings:
+        for slot, step in enumerate(order):
+            s = ring_index(place + step, sq)
+            remote(
+                xs[i].at[s, other], sib_x.at[i, slot], x_send.at[i, slot], x_recv.at[i, slot], "head", other
+            ).start()
+            copy = pltpu.make_async_copy(xs[i].at[s, me_head], own_x.at[i, slot], local.at[i, slot])
+            copy.start()
+            loads.append(copy)
+
+    def mine(k):
+        return (me + 1 + k) % sq
+
+    kinds = (
+        (lambda d, s: g3.at[:, d, s], v3, l3),
+        (lambda d, s: gb.at[d, s], vb, lb),
+        (lambda d, s: gd.at[d, s], vd, ld),
+    )
+
+    def share(k, carry):
+        s = mine(k)
+        for m, (src, own, land) in enumerate(kinds):
+            pltpu.make_async_copy(src(me_dp, s), own.at[k], local.at[2 + m, k]).start()
+            for d in range(1, dp):
+                peer = (me_dp + d) % dp
+                remote(
+                    src(peer, s), land.at[d - 1, k], d_send.at[m, d - 1, k], d_recv.at[m, d - 1, k], "dp", peer
+                ).start()
+        return carry
+
+    lax.fori_loop(0, sq, share, 0)
+
+    smalls = ((small, osmall), (sb, osb))
+
+    def tell(k, carry):
+        for d in range(dp):
+            for m, (src, dst) in enumerate(smalls):
+                remote(
+                    src, dst.at[me_head, me_dp, me], b_send.at[m, d, k], b_recv.at[m, d, k], ("dp", "seq"),
+                    ((me_dp + d) % dp, mine(k)),
+                ).start()
+        return carry
+
+    lax.fori_loop(0, sq - 1, tell, 0)
+    for d in range(1, dp):
+        for m, (src, dst) in enumerate(smalls):
+            remote(
+                src, dst.at[me_head, me_dp, me], b_send.at[m, d, sq - 1], b_recv.at[m, d, sq - 1],
+                ("dp", "seq"), ((me_dp + d) % dp, me),
+            ).start()
+    keep = [pltpu.make_async_copy(src, dst.at[me_head, me_dp, me], local.at[5, m]) for m, (src, dst) in enumerate(smalls)]
+    for copy in keep:
+        copy.start()
+
+    def ready(i, slot):
+        remote(
+            xs[i].at[me, other], sib_x.at[i, slot], x_send.at[i, slot], x_recv.at[i, slot], "head", other
+        ).wait_recv()
+        loads[i * sq + slot].wait()
+
+    def both(i, slot, h):
+        at = pl.ds(h * piece, piece)
+        return own_x[i, slot, at].astype(F32) + sib_x[i, slot, at].astype(F32)
+
+    def hop(i, t, h, to_right, src):
+        sends, recvs, buf, axis_at = (r_send, r_recv, rbuf, right) if to_right else (l_send, l_recv, lbuf, left)
+        return remote(src, sub(buf.at[i, t], h), sends.at[i, t, h], recvs.at[i, t, h], "seq", axis_at)
+
+    def start_fresh(i, slot, t, h, to_right):
+        at = pl.ds(h * piece, piece)
+        own_x[i, slot, at] = both(i, slot, h).astype(BF16)
+        hop(i, t, h, to_right, sub(own_x.at[i, slot], h)).start()
+
+    def pass_on(i, slot, t, h, to_right):
+        buf = rbuf if to_right else lbuf
+        at = pl.ds(h * piece, piece)
+        hop(i, t - 1, h, to_right, sub(buf.at[i, t - 1], h)).wait_recv()
+        buf[i, t - 1, at] = (buf[i, t - 1, at].astype(F32) + both(i, slot, h)).astype(BF16)
+        hop(i, t, h, to_right, sub(buf.at[i, t - 1], h)).start()
+
+    def give(k, carry):
+        s = mine(k)
+        for m, (src, own, land) in enumerate(kinds):
+            pltpu.make_async_copy(src(me_dp, s), own.at[k], local.at[2 + m, k]).wait()
+            total = own[k].astype(F32)
+            for d in range(1, dp):
+                peer = (me_dp + d) % dp
+                remote(
+                    src(peer, s), land.at[d - 1, k], d_send.at[m, d - 1, k], d_recv.at[m, d - 1, k], "dp", peer
+                ).wait_recv()
+                total = total + land[d - 1, k].astype(F32)
+            own[k] = total.astype(BF16)
+        return carry
+
+    def lane(s):
+        return pl.ds(pl.multiple_of(s * width, width), width)
+
+    def home(k, m, s_to, s_from):
+        src = (v3, vb, vd)[m].at[k]
+        dst = (o3.at[:, :, lane(s_from)], ob.at[me_head, s_from], od.at[s_from])[m]
+        return remote(src, dst, q_send.at[m, k], q_recv.at[m, k], "seq", s_to)
+
+    def give_away(k, carry):
+        give(k, carry)
+        for m in range(3):
+            home(k, m, mine(k), me).start()
+        return carry
+
+    def finish(i):
+        slot = sq - 1
+        ready(i, slot)
+        for h in range(parts):
+            at = pl.ds(h * piece, piece)
+            for to_right in (True, False):
+                buf = rbuf if to_right else lbuf
+                hop(i, half - 1, h, to_right, sub(buf.at[i, half - 1], h)).wait_recv()
+            total = both(i, slot, h) + rbuf[i, half - 1, at].astype(F32) + lbuf[i, half - 1, at].astype(F32)
+            fin[i, at] = total.astype(BF16)
+            dst = sub(outs[i].at[me_head], h)
+            pltpu.make_async_copy(sub(fin.at[i], h), dst, local.at[6 + i, h]).start()
+            remote(sub(fin.at[i], h), dst, f_send.at[i, h], f_recv.at[i, h], "head", other).start()
+
+    for t in range(half + 1):
+        for i in rings:
+            if t == 0:
+                ready(i, 0)
+                for h in first:
+                    start_fresh(i, 0, 0, h, True)
+                for h in second:
+                    start_fresh(i, 0, 0, h, False)
+            elif t < half:
+                ready(i, 2 * t - 1)
+                ready(i, 2 * t)
+                for h in range(parts):
+                    for to_right, slot, early in ((True, 2 * t - 1, first), (False, 2 * t, second)):
+                        if t == 1 and h not in early:
+                            start_fresh(i, slot, t, h, to_right)
+                        else:
+                            pass_on(i, slot, t, h, to_right)
+            else:
+                finish(i)
+        lax.fori_loop(t * (sq - 1) // (half + 1), (t + 1) * (sq - 1) // (half + 1), give_away, 0)
+    give(sq - 1, 0)
+    mine_home = [
+        pltpu.make_async_copy((v3, vb, vd)[m].at[sq - 1], dst, local.at[2 + m, sq])
+        for m, dst in enumerate((o3.at[:, :, lane(me)], ob.at[me_head, me], od.at[me]))
+    ]
+    for copy in mine_home:
+        copy.start()
+
+    def relay_bc(source, k):
+        return remote(
+            ob.at[me_head, source], ob.at[me_head, source], f_send.at[2, k], f_recv.at[2, k], "head", other
+        )
+
+    def relay_small(m, d, source, k):
+        ref = smalls[m][1].at[me_head, d, source]
+        return remote(ref, ref, b_send.at[2 + m, d, k], b_recv.at[2 + m, d, k], "head", other)
+
+    for copy in keep + mine_home:
+        copy.wait()
+    relay_bc(me, sq - 1).start()
+    for m in range(2):
+        relay_small(m, me_dp, me, sq - 1).start()
+
+    def came(k):
+        return (me + 2 * sq - 1 - k) % sq
+
+    def collect(k, carry):
+        for m in range(3):
+            home(k, m, mine(k), came(k)).wait()
+        relay_bc(came(k), k).start()
+        for d in range(dp):
+            frm = (me_dp + dp - d) % dp
+            for m, (src, dst) in enumerate(smalls):
+                remote(
+                    src, dst.at[me_head, frm, came(k)], b_send.at[m, d, k], b_recv.at[m, d, k], ("dp", "seq"),
+                    ((me_dp + d) % dp, mine(k)),
+                ).wait()
+                relay_small(m, frm, came(k), k).start()
+        return carry
+
+    lax.fori_loop(0, sq - 1, collect, 0)
+    for d in range(1, dp):
+        frm = (me_dp + dp - d) % dp
+        for m, (src, dst) in enumerate(smalls):
+            remote(
+                src, dst.at[me_head, frm, me], b_send.at[m, d, sq - 1], b_recv.at[m, d, sq - 1], ("dp", "seq"),
+                ((me_dp + d) % dp, me),
+            ).wait()
+            relay_small(m, frm, me, sq - 1).start()
+
+    def settle(k, carry):
+        relay_bc(came(k), k).wait_send()
+        remote(
+            ob.at[me_head, came(k)], ob.at[other, came(k)], f_send.at[2, k], f_recv.at[2, k], "head", other
+        ).wait_recv()
+        for d in range(dp):
+            for m in range(2):
+                relay_small(m, d, came(k), k).wait_send()
+                ref = smalls[m][1].at[other, d, came(k)]
+                remote(ref, ref, b_send.at[2 + m, d, k], b_recv.at[2 + m, d, k], "head", other).wait_recv()
+        for m, (src, own, land) in enumerate(kinds):
+            for d in range(1, dp):
+                peer = (me_dp + d) % dp
+                remote(
+                    src(peer, mine(k)), land.at[d - 1, k], d_send.at[m, d - 1, k], d_recv.at[m, d - 1, k], "dp", peer
+                ).wait_send()
+        return carry
+
+    lax.fori_loop(0, sq, settle, 0)
+    for i in rings:
+        for slot in range(sq):
+            remote(
+                xs[i].at[me, other], sib_x.at[i, slot], x_send.at[i, slot], x_recv.at[i, slot], "head", other
+            ).wait_send()
+        for t in range(half):
+            for h in range(parts):
+                for to_right, early in ((True, first), (False, second)):
+                    if t > 0 or h in early:
+                        hop(i, t, h, to_right, sub(own_x.at[i, 0], h)).wait_send()
+        for h in range(parts):
+            src = sub(fin.at[i], h)
+            pltpu.make_async_copy(src, sub(outs[i].at[me_head], h), local.at[6 + i, h]).wait()
+            copy = remote(src, sub(outs[i].at[other], h), f_send.at[i, h], f_recv.at[i, h], "head", other)
+            copy.wait_send()
+            copy.wait_recv()
+
+
+def scatter_all(x0, x1, g3, gb, gd, small, sb, collective_id=1, parts=2):
+    dp, sq, hd = lax.axis_size("dp"), lax.axis_size("seq"), lax.axis_size("head")
+    _, _, rows, model = x0.shape
+    kinds, _, _, depth, width = g3.shape
+    anywhere = pl.BlockSpec(memory_space=pl.ANY)
+    dma = pltpu.SemaphoreType.DMA
+    S = jax.ShapeDtypeStruct
+    V = pltpu.VMEM
+    half = sq // 2
+    return pl.pallas_call(
+        functools.partial(scatter_kernel, parts),
+        out_shape=[
+            S((hd, rows, model), BF16), S((hd, rows, model), BF16), S((kinds, depth, sq * width), BF16),
+            S((hd, sq) + gb.shape[2:], BF16), S((sq,) + gd.shape[2:], BF16),
+            S((hd, dp, sq) + small.shape, F32), S((hd, dp, sq) + sb.shape, F32),
+        ],
+        in_specs=[anywhere] * 7,
+        out_specs=[anywhere] * 7,
+        scratch_shapes=[
+            V((2, sq, rows, model), BF16), V((2, sq, rows, model), BF16),
+            V((2, half, rows, model), BF16), V((2, half, rows, model), BF16), V((2, rows, model), BF16),
+            V((sq, kinds, depth, width), BF16), V((sq,) + gb.shape[2:], BF16), V((sq,) + gd.shape[2:], BF16),
+            V((dp - 1, sq, kinds, depth, width), BF16), V((dp - 1, sq) + gb.shape[2:], BF16),
+            V((dp - 1, sq) + gd.shape[2:], BF16),
+            dma((8, sq + 1)), dma((2, sq)), dma((2, sq)),
+            dma((2, half, parts)), dma((2, half, parts)), dma((2, half, parts)), dma((2, half, parts)),
+            dma((3, max(parts, sq))), dma((3, max(parts, sq))),
+            dma((3, dp, sq)), dma((3, dp, sq)), dma((3, sq)), dma((3, sq)), dma((4, dp, sq)), dma((4, dp, sq)),
+        ],
+        compiler_params=pltpu.CompilerParams(
+            collective_id=collective_id, has_side_effects=True, vmem_limit_bytes=56 << 20
+        ),
+    )(x0, x1, g3, gb, gd, small, sb)
+
+
+def total_kernel(x, o, land, send, recv):
+    here = axes_here()
+    (me, sq), (me_head, hd) = here["seq"], here["head"]
+    barrier = pltpu.get_barrier_semaphore()
+    count = sq * hd
+    flat = me * hd + me_head
+
+    def peer(k):
+        to = (flat + 1 + k) % count
+        return {"seq": to // hd, "head": to % hd}
+
+    def hello(k, carry):
+        pl.semaphore_signal(barrier, inc=1, device_id=peer(k), device_id_type=pl.DeviceIdType.MESH)
+        return carry
+
+    lax.fori_loop(0, count - 1, hello, 0)
+    pl.semaphore_wait(barrier, count - 1)
+
+    def copy(k):
+        return pltpu.make_async_remote_copy(
+            src_ref=x, dst_ref=land.at[k], send_sem=send.at[k], recv_sem=recv.at[k],
+            device_id=peer(k), device_id_type=pl.DeviceIdType.MESH,
+        )
+
+    def start(k, carry):
+        copy(k).start()
+        return carry
+
+    lax.fori_loop(0, count - 1, start, 0)
+    o[...] = x[...]
+
+    def take(k, carry):
+        copy(k).wait()
+        o[...] += land[k]
+        return carry
+
+    lax.fori_loop(0, count - 1, take, 0)
+
+
+def total_over_heads(x, collective_id):
+    count = lax.axis_size("seq") * lax.axis_size("head")
+    vmem = pl.BlockSpec(memory_space=pltpu.VMEM)
+    dma = pltpu.SemaphoreType.DMA
+    return pl.pallas_call(
+        total_kernel,
+        out_shape=jax.ShapeDtypeStruct(x.shape, x.dtype),
+        in_specs=[vmem],
+        out_specs=vmem,
+        scratch_shapes=[pltpu.VMEM((count - 1,) + x.shape, x.dtype), dma((count - 1,)), dma((count - 1,))],
+        compiler_params=pltpu.CompilerParams(collective_id=collective_id, has_side_effects=True),
+    )(x)
+
+
+def project_kernel(normed, cot, w3, wb, wd, p_ref, gs_ref):
+    width = w3.shape[2]
+    at = 0
+    for weight in (w3.at[0], w3.at[1], wb, wd):
+        cols = weight.shape[1]
+        p_ref[:, at : at + cols] = mm(normed[...], weight[...]).astype(BF16)
+        at += cols
+    gs_ref[...] = mm(cot[...], w3[2])
+
+
+def project(normed, cot, w3, wb, wd):
+    rows, model = normed.shape
+    width, tile = w3.shape[2], 256
+    cols = 2 * width + wb.shape[1] + wd.shape[1]
+    row_block = lambda n: pl.BlockSpec((tile, n), lambda i: (i, 0))
+    return pl.pallas_call(
+        project_kernel,
+        grid=(rows // tile,),
+        in_specs=[row_block(model), row_block(model)] + [whole_block(a) for a in (w3, wb, wd)],
+        out_specs=[row_block(cols), row_block(width)],
+        out_shape=[jax.ShapeDtypeStruct((rows, cols), BF16), jax.ShapeDtypeStruct((rows, width), F32)],
+        compiler_params=pltpu.CompilerParams(vmem_limit_bytes=56 << 20),
+    )(normed, cot, w3, wb, wd)
+
+
+def product_kernel(normed, cot, g, scaled, w3, wb, wd, branch, gn, g3, gb, gd, gnorm):
+    width = w3.shape[2]
+    n, c = normed[...], cot[...]
+    branch[...] = mm(scaled[...], w3[2], NT).astype(BF16)
+    g3[2] = mm(c, scaled[...], TN).astype(BF16)
+    at = 0
+    total = jnp.zeros(gn.shape, F32)
+    dots = jnp.zeros(gnorm.shape, F32)
+    for i, weight in enumerate((w3.at[0], w3.at[1], wb, wd)):
+        cols = weight.shape[1]
+        part = g[:, at : at + cols]
+        at += cols
+        total = total + mm(part, weight[...], NT)
+        if i < 3:
+            grad = mm(n, part, TN)
+            if i < 2:
+                g3[i] = grad.astype(BF16)
+            else:
+                gb[...] = grad.astype(BF16)
+            dots = dots + mm_left(jnp.ones((8, cols), BF16), grad * weight[...].astype(F32), 2, NT)
+        else:
+            grad = mm(part, n, TN)
+            gd[...] = grad[:16].astype(BF16)
+            dots = dots + jnp.sum(grad * weight[...].astype(F32).T, axis=0, keepdims=True)
+    gn[...] = total.astype(BF16)
+    gnorm[...] = dots
+
+
+def products(normed, cot, g, scaled, w3, wb, wd):
+    rows, model = normed.shape
+    width, tile = w3.shape[2], 256
+    col_block = lambda n: pl.BlockSpec((n, tile), lambda j: (0, j))
+    row_block = lambda n: pl.BlockSpec((tile, n), lambda j: (j, 0))
+    three = pl.BlockSpec((3, tile, width), lambda j: (0, j, 0))
+    S = jax.ShapeDtypeStruct
+    return pl.pallas_call(
+        product_kernel,
+        grid=(model // tile,),
+        in_specs=[col_block(rows), col_block(rows), whole_block(g), whole_block(scaled), three,
+                  row_block(wb.shape[1]), row_block(wd.shape[1])],
+        out_specs=[col_block(rows), col_block(rows), three, row_block(wb.shape[1]), col_block(16), col_block(8)],
+        out_shape=[
+            S((rows, model), BF16), S((rows, model), BF16), S(w3.shape, BF16), S(wb.shape, BF16),
+            S((16, model), BF16), S((8, model), F32),
+        ],
+        compiler_params=pltpu.CompilerParams(vmem_limit_bytes=60 << 20),
+    )(normed, cot, g, scaled, w3, wb, wd)
+
+
 def rms(x, gain):
     return x * lax.rsqrt(jnp.mean(x * x, axis=-1, keepdims=True) + EPSILON) * gain
 
@@ -347,19 +990,18 @@
     tokens, norm_gain, w_gate_in, w_x_in, w_bc_in, w_dt_in, conv_x_w, conv_x_b, conv_bc_w, conv_bc_b,
     dt_bias, a_log, d_skip, gate_gain, w_out, prefix_len, cotangent,
 ):
-    sq, hd = lax.axis_size("seq"), lax.axis_size("head")
+    dp, sq, hd = lax.axis_size("dp"), lax.axis_size("seq"), lax.axis_size("head")
     me_seq, me_head = lax.axis_index("seq"), lax.axis_index("head")
     micro, seqs, span, model = tokens.shape
     group = micro * seqs
     rows_here = group * span
     own_rows = rows_here // hd
-    half = w_x_in.shape[1]
+    depth, half = w_x_in.shape
     width = half // sq
     heads = w_dt_in.shape[1] // sq
     state = w_bc_in.shape[1] // 2
     full_inner = half * hd
     prefix = prefix_len.reshape(group)
-    everyone = ("seq", "head")
 
     def mine(x):
         return lax.dynamic_slice_in_dim(x.reshape(rows_here, model), me_head * own_rows, own_rows, 0)
@@ -367,26 +1009,15 @@
     def blocks(x):
         return x.reshape(sq, group, span, -1)
 
-    my_tokens = mine(tokens).astype(F32)
-    my_cot = mine(cotangent)
-    normed = lax.all_gather(rms(my_tokens, norm_gain).astype(BF16), everyone, axis=0, tiled=True)
-
-    def columns(w):
-        return lax.all_gather(
-            lax.all_to_all(w, "seq", split_axis=1, concat_axis=0, tiled=True), "dp", axis=0, tiled=True
-        )
-
-    wd = lax.dynamic_slice_in_dim(
-        lax.all_gather(w_dt_in, ("dp", "seq"), axis=0, tiled=True), me_seq * heads, heads, 1
-    )
-    wb = lax.all_gather(w_bc_in, ("dp", "seq"), axis=0, tiled=True)
-    wcat = jnp.concatenate(
-        [columns(w_gate_in), columns(w_x_in), wb, jnp.pad(wd, ((0, 0), (0, 128 - heads)))], axis=1
-    )
-    wo = lax.all_gather(
-        lax.all_to_all(w_out, "seq", split_axis=0, concat_axis=1, tiled=True), "dp", axis=1, tiled=True
-    )
-    cot = lax.all_gather(my_cot, everyone, axis=0, tiled=True)
+    w3 = jnp.stack([w_gate_in, w_x_in, w_out.T])
+    wd = jnp.pad(w_dt_in.T.reshape(sq, heads, depth), ((0, 0), (0, 16 - heads), (0, 0)))
+    normed_own = rms(mine(tokens).astype(F32), norm_gain).astype(BF16)
+    normed, cot, w3, wb, wd = gather_all(normed_own, mine(cotangent), w3, w_bc_in, wd, 0)
+    normed = normed.reshape(sq * rows_here, model)
+    cot = cot.reshape(sq * rows_here, model)
+    w3 = w3.reshape(3, model, width)
+    wb = wb.reshape(model, 2 * state)
+    wd = jnp.pad(wd.transpose(0, 1, 3, 2).reshape(model, 16), ((0, 0), (0, 112)))
 
     def part(x, size, axis):
         return lax.dynamic_slice_in_dim(x, me_seq * size, size, axis)
@@ -398,55 +1029,43 @@
         part(conv_x_w, width, 1), part(conv_x_b, width, 0)[None], conv_bc_w, conv_bc_b[None],
         spread(dt_bias), spread(-jnp.exp(a_log)), spread(d_skip), part(gate_gain, width, 0)[None],
     )
-    p = blocks(jnp.dot(normed, wcat, preferred_element_type=F32).astype(BF16))
-    gs = blocks(jnp.einsum("rd,kd->rk", cot, wo, preferred_element_type=F32))
+    p, gs = (blocks(a) for a in project(normed, cot, w3, wb, wd))
     *saved, sums = ssd_forward(heads, state, prefix, p, gs, params)
-    totals = lax.psum(sums, everyone)
+    totals = total_over_heads(sums, 1)
     g, scaled, small, smallbc = ssd_backward(heads, state, full_inner, prefix, p, gs, saved, totals, params)
-    g = g.reshape(sq * rows_here, -1)
-    scaled = scaled.reshape(sq * rows_here, width)
-    branch = lax.psum_scatter(
-        jnp.dot(scaled, wo, preferred_element_type=F32).astype(BF16), everyone, scatter_dimension=0, tiled=True
+    branch, gn, g3, gb, gd, gnorm = products(
+        normed, cot, g.reshape(sq * rows_here, -1), scaled.reshape(sq * rows_here, width), w3, wb, wd
     )
-    result_own = (my_tokens + branch.astype(F32)).astype(BF16)
-    part_normed = jnp.einsum("rc,kc->rk", g, wcat, preferred_element_type=F32)
-    grad_normed = lax.psum_scatter(
-        part_normed.astype(BF16), everyone, scatter_dimension=0, tiled=True
-    ).astype(F32)
-    gw = jnp.einsum("rk,rc->kc", normed, g, preferred_element_type=F32)
-    g_wo = jnp.einsum("rk,rd->kd", scaled, cot, preferred_element_type=F32)
-    grad_norm = jnp.sum(gw * wcat.astype(F32), axis=1) / norm_gain
-    _, pull_norm = jax.vjp(lambda x: rms(x, norm_gain), my_tokens)
-    grad_own = my_cot.astype(F32) + pull_norm(grad_normed)[0]
-
-    def home(x):
-        return lax.all_to_all(
-            lax.psum_scatter(x, "dp", scatter_dimension=0, tiled=True),
-            "seq", split_axis=0, concat_axis=1, tiled=True,
-        )
-
-    g_gate, g_x = (home(gw[:, at : at + width].astype(BF16)).astype(F32) for at in (0, width))
-    g_dt = home(gw[:, 2 * width + 2 * state :][:, :heads])
-    g_bc = lax.psum_scatter(
-        lax.psum(gw[:, 2 * width : 2 * width + 2 * state], "head"), ("dp", "seq"), scatter_dimension=0, tiled=True
+    by_head = small[6:9].reshape(3, heads, width // heads)
+    per_head = jnp.concatenate([by_head[:2, :, 0], jnp.sum(by_head[2:], axis=2)], axis=0).reshape(1, 3 * heads)
+    small = jnp.concatenate(
+        [small[:6], jnp.pad(per_head, ((0, 0), (0, width - 3 * heads))), jnp.zeros((1, width), F32)], axis=0
     )
-    g_out = lax.all_to_all(
-        lax.psum_scatter(g_wo.astype(BF16), "dp", scatter_dimension=1, tiled=True),
-        "seq", split_axis=1, concat_axis=0, tiled=True,
-    ).astype(F32)
-
-    def whole(x):
-        return lax.all_gather(x, "head", axis=0, tiled=True).reshape(micro, seqs, span, model)
-
-    def per_head(x):
-        return x.reshape(heads, width // heads)
-
-    small = lax.all_gather(lax.psum(small, "dp"), "seq", axis=1, tiled=True)
-    s_norm, s_bc = lax.psum((grad_norm, smallbc), ("dp", "seq", "head"))
-    by_head = small.reshape(16, sq * heads, width // heads)
+    wide = jnp.concatenate([smallbc, (gnorm[0] / norm_gain).reshape(8, model // 8)], axis=0)
+    to_own = lambda x: x.reshape(sq, hd, own_rows, model)
+    branch, gn, o3, ob, od, small, wide = scatter_all(
+        to_own(branch), to_own(gn), g3.reshape(3, dp, sq, depth, width), gb.reshape(dp, sq, depth, 2 * state),
+        gd.reshape(16, dp, sq, depth).transpose(1, 2, 0, 3), small, wide, 2,
+    )
+
+    def natural(x):
+        return x.reshape(tokens.shape)
+
+    x = tokens.astype(F32)
+    result = (x + natural(branch).astype(F32)).astype(BF16)
+    _, pull_norm = jax.vjp(lambda v: rms(v, norm_gain), x)
+    grad_tokens = cotangent.astype(F32) + pull_norm(natural(gn).astype(F32))[0]
+    o3 = o3.astype(F32)
+    g_bc = jnp.sum(ob.astype(F32), axis=(0, 1))
+    g_dt = od[:, :heads].transpose(2, 0, 1).reshape(depth, sq * heads).astype(F32)
+    small = jnp.sum(lax.dynamic_index_in_dim(small, me_head, 0, False), axis=0)
+    wide = jnp.sum(wide, axis=(0, 1, 2))
+    lanes = lambda a: a.swapaxes(0, 1).reshape(a.shape[1], half)
+    g_channel = lanes(small)
+    g_head = small[:, 6, : 3 * heads].reshape(sq, 3, heads).swapaxes(0, 1).reshape(3, sq * heads)
     return (
-        whole(result_own), whole(grad_own), s_norm, g_gate, g_x, g_bc, g_dt,
-        small[:4], small[4], s_bc[:4], s_bc[4], by_head[6, :, 0], by_head[7, :, 0], by_head[8].sum(-1), small[5], g_out,
+        result, grad_tokens, wide[8:].reshape(model), o3[0], o3[1], g_bc, g_dt,
+        g_channel[:4], g_channel[4], wide[:4], wide[4], g_head[0], g_head[1], g_head[2], g_channel[5], o3[2].T,
     )
 
 

time: 986 us -> 445 us (0.45)
  waiting for transfers between devices: 625 us -> 0 us
  Pallas kernels: 60.3 us -> 405 us
  blocking collectives: 131 us -> 0 us
  matrix products: 59.3 us -> 0 us
  starting transfers between devices: 36.9 us -> 0 us
  local copies, waits for them, and re-layouts: 48.9 us -> 22.2 us
  between operations: 14.2 us -> 0.87 us
    pallas_call x0 -> x5, Pallas kernels: none -> 345 us  [the longest x1 152 us: scatter_all(): pl.pallas_call(functools.partial(scatter_kernel, parts), out_shape=[S((hd...]
    reduce_scatter x6 -> x0, waiting for transfers between devices: 310 us -> none  [the longest x1 123 us: body(): lax.psum_scatter(part_normed.astype(BF16), everyone, scatter_dimension=0,...]
    all_gather x8 -> x0, waiting for transfers between devices: 189 us -> none  [the longest x1 76.2 us: body(): lax.all_gather(rms(my_tokens, norm_gain).astype(BF16), everyone, axis=0,...]
    psum x2 -> x0, waiting for transfers between devices: 82.9 us -> none  [the longest x1 82.9 us: body(): totals = lax.psum(sums, everyone)]
    all_gather x2 -> x0, blocking collectives: 59.7 us -> none  [the longest x1 36.5 us: body(): lax.all_gather(w_dt_in, ('dp', 'seq'), axis=0, tiled=True)]
    dot_general x6 -> x0, matrix products: 59.3 us -> none  [the longest x1 13.4 us: body(): gw = jnp.einsum('rk,rc->kc', normed, g, preferred_element_type=F32)]
    psum x2 -> x0, blocking collectives: 54.7 us -> none  [the longest x1 49 us: body(): s_norm, s_bc = lax.psum((grad_norm, smallbc), ('dp', 'seq', 'head'))]
    all_to_all x6 -> x0, starting transfers between devices: 35.8 us -> none  [the longest x3 16.4 us: home(): lax.all_to_all(lax.psum_scatter(x, 'dp', scatter_dimension=0, tiled=True)...]
  transfers between devices with their start and end apart: 23 -> 0, of which waited for: 15 -> 0; matrix products, arithmetic and copies ran while one was open for 8% -> 0% of each run, Pallas kernels for 0% -> 0%
where the time goes in v3:
time: 445 us; the launch traced here: 442 us
  Pallas kernels  405 us (91%)
  local copies, waits for them, and re-layouts  22.2 us (5%)
  other arithmetic  13.4 us (3%)
    pallas_call x1, Pallas kernels, scatter_all(): pl.pallas_call(functools.partial(scatter_kernel, parts), out_shape=[S((hd...  152 us
    pallas_call x1, Pallas kernels, gather_all(): pl.pallas_call(gather_kernel, out_shape=[S((sq, hd, rows, model), BF16),...  133 us
    pallas_call x1, Pallas kernels, ssd_backward(): pl.pallas_call(functools.partial(backward_kernel, heads, state, full_inne...  35.4 us
    pallas_call x1, Pallas kernels, products(): pl.pallas_call(product_kernel, grid=(model // tile,), in_specs=[col_block...  33.3 us
    pallas_call x1, Pallas kernels, ssd_forward(): pl.pallas_call(functools.partial(forward_kernel, heads, state), grid=(gro...  24.9 us
    pallas_call x1, Pallas kernels, project(): pl.pallas_call(project_kernel, grid=(rows // tile,), in_specs=[row_block(...  17.1 us
    pallas_call x1, Pallas kernels, total_over_heads(): pl.pallas_call(total_kernel, out_shape=jax.ShapeDtypeStruct(x.shape, x.dt...  9.86 us

profile of v3, /device:TPU:19, one launch (start us, length us, event | category | flops | bytes accessed | tf_op | source)
XLA Modules:
  0.0 441.7 jit_solution(5429931570005477794)
XLA Ops:
  0.6 0.0 copy-start
  0.7 1.3 fusion.5
  2.1 2.0 fusion.7.own_a
  4.1 1.9 constant_dynamic-slice_fusion.1.own_b
  6.0 0.2 copy.59
  6.2 1.3 pad_maximum_fusion.w3
  7.5 0.6 pad.12.wd
  8.2 132.8 %shard_map.288 = (bf16[8,2,128,2048]{3,2,1,0:T(8,128)(2,1)}, bf16[8,2,128,2048]{3,2,1,0:T(8,128)(2,1)}, bf16[3,2,8,128,256]{4,3,2,1,0:T(8,128)(2,1)}, bf16[2,8,1...) custom-call(bf16[128,2048]{1,0:T(8,128)(2,1)} %fusion.7.own_a, bf16[128,2048]{1,0:T(8,128)(2,1)} %constant_dynamic-slice_fusion.1.own_b, ...), custom_call_target="tpu_custom_call" | custom-call | tf_op jit(solution)/shard_map/pallas_call | solution.py:548
  141.0 1.1 copy.60
  142.1 0.9 pad.13.wd
  143.0 17.1 %shard_map.289 = (bf16[2048,896]{1,0:T(8,128)(2,1)}, f32[2048,256]{1,0:T(8,128)}) custom-call(bf16[2048,2048]{1,0:T(8,128)(2,1)} %bitcast.78, bf16[2048,2048]{1,0:T(8,128)(2,1)} %bitcast.80, bf16[3,2048,256]{2,1,0:T(8,128)(2,1)} %bitcast.84, bf16[2048,256]{1,0:T(8,128)(2,1)} %bitcast.92, bf16[2048,128]{1,0:T(8,128)(2,1)} %pad.13.wd), custom_call_target="tpu_custom_call" | custom-call | tf_op jit(solution)/shard_map/pallas_call | solution.py:926
  160.1 0.1 dynamic_slice.33
  160.1 0.1 broadcast_in_dim.32
  160.2 0.6 broadcast_in_dim_reshape.10.nega
  160.9 0.6 constant_dynamic-slice_fusion.cxw
  161.5 0.1 dynamic_slice.34
  161.5 0.1 broadcast_in_dim.33
  161.6 0.6 broadcast_in_dim_reshape.11.dsk
  162.3 0.1 dynamic_slice.32
  162.3 0.1 broadcast_in_dim.31
  162.4 0.6 broadcast_in_dim_reshape.9.dtb
  163.0 1.3 dynamic_slice.31
  164.4 1.3 dynamic_slice.35
  165.7 24.9 %shard_map.290 = (f32[8,2,128,256]{3,2,1,0:T(8,128)}, f32[8,2,128,256]{3,2,1,0:T(8,128)}, f32[8,2,128,256]{3,2,1,0:T(8,128)}, f32[8,2,128,256]{3,2,1,0:T(8,128)}...) custom-call(s32[2]{0:T(128)} %bitcast.124, ...), custom_call_target="tpu_custom_call" | custom-call | tf_op jit(solution)/shard_map/pallas_call | solution.py:311
  190.6 9.9 %shard_map.291.tot_ref = f32[2,2,8,128]{3,2,1,0:T(8,128)} custom-call(f32[2,2,8,128]{3,2,1,0:T(8,128)} %get-tuple-element.62.x), custom_call_target="tpu_custom_call" | custom-call | tf_op jit(solution)/shard_map/pallas_call | solution.py:901
  200.4 35.4 %shard_map.292 = (bf16[8,2,128,896]{3,2,1,0:T(8,128)(2,1)}, bf16[8,2,128,256]{3,2,1,0:T(8,128)(2,1)}, f32[16,256]{1,0:T(8,128)}, f32[8,256]{1,0:T(8,128)}) custom-call(s32[2]{0:T(128)} %bitcast.125, bf16[8,2,128,896]{3,2,1,0:T(8,128)(2,1)} %bitcast.83, f32[8,2,128,256]{3,2,1,0:T(8,128)} %bitcast.91, f32[8,2,128,256]{3,2,1,0:T(8,128)} %get-tuple-element.55.xc_ref, ...), custom_call_target="tpu_custom_call" | custom-call | tf_op jit(solution)/shard_map/pallas_call | solution.py:327
  235.8 0.0 copy-start.11
  235.8 0.0 copy-start.15
  235.8 0.0 copy-start.13
  235.8 33.3 %shard_map.293 = (bf16[2048,2048]{1,0:T(8,128)(2,1)}, bf16[2048,2048]{1,0:T(8,128)(2,1)}, bf16[3,2048,256]{2,1,0:T(8,128)(2,1)}, bf16[2048,256]{1,0:T(8,128)(2,1...) custom-call(bf16[2048,2048]{1,0:T(8,128)(2,1)} %bitcast.79, bf16[2048,2048]{1,0:T(8,128)(2,1)} %bitcast.81, ...), custom_call_target="tpu_custom_call" | custom-call | tf_op jit(solution)/shard_map/pallas_call | solution.py:971
  269.2 0.8 slice.74
  270.1 0.6 pad_maximum_fusion.1.sb
  270.7 0.1 reshape.182
  270.8 0.1 copy.71
  270.9 0.1 slice.73
  271.0 0.1 reduce_sum.70
  271.1 0.1 reshape.183
  271.2 0.1 pad.19.clone
  271.3 0.7 fusion.9.small
  271.9 0.8 copy.72
  272.8 0.6 copy.75
  273.4 151.9 %shard_map.294 = (bf16[2,128,2048]{2,1,0:T(8,128)(2,1)}, bf16[2,128,2048]{2,1,0:T(8,128)(2,1)}, bf16[3,128,2048]{2,1,0:T(8,128)(2,1)}, bf16[2,8,128,256]{3,2,1,0...) custom-call(bf16[8,2,128,2048]{3,2,1,0:T(8,128)(2,1)} %bitcast.88, ...), custom_call_target="tpu_custom_call" | custom-call | tf_op jit(solution)/shard_map/pallas_call | solution.py:832
  425.4 1.8 convert_element_type.54
  427.2 1.5 slice_bitcast_fusion
  428.7 1.3 copy.70
  430.0 0.6 copy-done.3
  430.6 0.6 fusion.3
  431.2 0.1 copy-done.4
  431.3 0.3 copy-done.5
  431.6 2.7 fusion.1
  434.4 0.8 convert_reduce_fusion
  435.2 0.6 slice.94
  435.8 0.1 copy.64
  435.9 0.1 copy.65
  436.0 0.6 squeeze.41
  436.6 0.1 copy.66
  436.7 0.6 squeeze.42
  437.3 0.1 copy.67
  437.3 0.6 squeeze.43
  437.9 0.6 fusion.12
  438.6 0.6 copy.73
  439.2 0.6 slice.96
  439.8 0.6 slice.97
  440.4 1.3 slice_convert_fusion
  (47 shorter events, 0.2 us)
Async XLA Ops:
  0.6 160.2 %copy-start = (f32[4,2048]{1,0:T(4,128)S(1)}, f32[4,2048]{1,0:T(4,128)}, u32[]{:S(2)}) copy-start(f32[4,2048]{1,0:T(4,128)} %param.23) | copy-start | bytes 98308
  0.7 5.3 %copy-start.8 = (bf16[2048,128]{1,0:T(8,128)(2,1)S(1)}, bf16[2048,128]{1,0:T(8,128)(2,1)}, u32[]{:S(2)}) copy-start(bf16[2048,128]{1,0:T(8,128)(2,1)} %param.31) | copy-start | bytes 1572868
  0.7 5.5 %copy-start.10 = (bf16[128,2048]{1,0:T(8,128)(2,1)S(1)}, bf16[128,2048]{1,0:T(8,128)(2,1)}, u32[]{:S(2)}) copy-start(bf16[128,2048]{1,0:T(8,128)(2,1)} %param.19) | copy-start | bytes 1572868
  0.7 5.5 %copy-start.9 = (bf16[128,2048]{1,0:T(8,128)(2,1)S(1)}, bf16[128,2048]{1,0:T(8,128)(2,1)}, u32[]{:S(2)}) copy-start(bf16[128,2048]{1,0:T(8,128)(2,1)} %param.20) | copy-start | bytes 1572868
  6.0 1.6 copy-start.14
  143.0 17.1 %copy-start.16 = (f32[32]{0:T(128)S(1)}, f32[32]{0:T(128)}, u32[]{:S(2)}) copy-start(f32[32]{0:T(128)} %param.28) | copy-start | bytes 388
  143.0 18.5 %copy-start.17 = (f32[32]{0:T(128)S(1)}, f32[32]{0:T(128)}, u32[]{:S(2)}) copy-start(f32[32]{0:T(128)} %param.29) | copy-start | bytes 388
  143.0 19.3 %copy-start.18 = (f32[32]{0:T(128)S(1)}, f32[32]{0:T(128)}, u32[]{:S(2)}) copy-start(f32[32]{0:T(128)} %param.27) | copy-start | bytes 388
  235.8 34.2 %copy-start.11 = (f32[2048]{0:T(1024)S(1)}, f32[2048]{0:T(1024)}, u32[]{:S(2)}) copy-start(f32[2048]{0:T(1024)} %param.18) | copy-start | bytes 24580
  235.8 34.2 %copy-start.15 = (f32[8,256]{1,0:T(8,128)S(1)}, f32[8,256]{1,0:T(8,128)}, u32[]{:S(2)}) copy-start(f32[8,256]{1,0:T(8,128)} %get-tuple-element.71) | copy-start | bytes 24580
  235.8 34.8 %copy-start.13 = (f32[16,256]{1,0:T(8,128)S(1)}, f32[16,256]{1,0:T(8,128)}, u32[]{:S(2)}) copy-start(f32[16,256]{1,0:T(8,128)} %get-tuple-element.70) | copy-start | bytes 49156
  428.7 1.3 copy-start.2
  428.7 1.9 copy-start.3
  430.0 1.3 copy-start.4
  430.0 1.6 copy-start.5
  431.6 2.7 copy-start.6
  431.6 3.5 copy-start.12
  431.6 6.9 %copy-start.7 = (f32[2,2,8,16,256]{4,3,2,1,0:T(8,128)S(1)}, f32[2,2,8,16,256]{4,3,2,1,0:T(8,128)}, u32[]{:S(2)}) copy-start(f32[2,2,8,16,256]{4,3,2,1,0:T(8,128)} %get-tuple-element.75) | copy-start | bytes 1572868
  431.6 10.1 %copy-start.1 = (f32[4,2048]{1,0:T(4,128)S(1)}, f32[4,2048]{1,0:T(4,128)}, u32[]{:S(2)}) copy-start(f32[4,2048]{1,0:T(4,128)} %param.23) | copy-start | bytes 98308
